TPU v7x, 512 devices: a whole 4x4x16 slice. The times are simulated.
512 devices in a mesh: mem: 32 (over y, z_lo), tile: 16 (over z_hi, x, core).
Axes of the slice: x: 4, y: 4, z: 16 (z_hi: 2, z_lo: 8; z = z_hi * 8 + z_lo), core: 2. Of those that a mesh axis runs over, the one named last changes fastest.
Arguments:
- ssh_prior: float32 [64, 256, 1024], P('mem', 'tile'), may hold values from -6 to 6
- ssh_forcing: float32 [64, 256, 1024], P('mem', 'tile'), may hold values from -6 to 6
- level_state: float32 [64, 8, 256, 1024], P('mem', None, 'tile'), may hold values from -6 to 6
- depth: float32 [256, 1024], P('tile'), may hold values from 0.5 to 4
- damping: float32 [256, 1024], P('tile'), may hold values from 0.02 to 0.5
- land_mask: int32 [256, 1024], P('tile'), may hold values 0 or 1
- obs_column: int32 [32, 16, 4, 128], P('mem', 'tile'), may hold values from 0 to 127
- obs_value: float32 [32, 16, 4, 128], P('mem', 'tile'), may hold values from -6 to 6
- obs_weight: float32 [32, 16, 4, 128], P('mem', 'tile'), may hold values from 0.2 to 5
- obs_count: int32 [32, 16, 4], P('mem', 'tile'), may hold values from 0 to 128, as said below
Outputs:
- ssh_analysis: float32 [64, 256, 1024], P('mem', 'tile')
- level_analysis: float32 [64, 8, 256, 1024], P('mem', None, 'tile')
Inputs may be any that keep to these rules, and one draw needn't show every extreme that they name: `obs_count`: in every draw one block has exactly 128 live slots and another has none.
All inputs are finite; a program needn't handle non-finite values. No bound on the sum of `land_mask` on one device may be relied on, other than what follows from the above.
Results may differ from a plain program's by a relative error of at most 0.0003.
Values sent between devices are 32-bit elements; how exact they have to be, the bound alone decides.
A program may use at most 64 MiB of HBM per device.

v0:
```python
import jax
import jax.numpy as jnp
from jax import lax
from jax.sharding import PartitionSpec as P

ITERS = 8
NS_STEPS = 8


precise = lax.Precision.HIGHEST


def extended(cells, sides, width):
    for axis, dim in sides:
        count = lax.axis_size(axis)
        ends = count - 1
        head = lax.slice_in_dim(cells, 0, width, axis=dim)
        tail = lax.slice_in_dim(cells, cells.shape[dim] - width, cells.shape[dim], axis=dim)
        cells = jnp.concatenate(
            [
                lax.ppermute(tail, axis, [(i, (i + 1) % count) for i in range(ends)]),
                cells,
                lax.ppermute(head, axis, [((i + 1) % count, i) for i in range(ends)]),
            ],
            axis=dim,
        )
    return cells


def face_weights(wet_pad):
    centre = wet_pad[..., 1:-1, :]
    north_face = jnp.sqrt(centre * wet_pad[..., :-2, :])
    south_face = jnp.sqrt(centre * wet_pad[..., 2:, :])
    east_face = jnp.sqrt(centre * jnp.roll(centre, -1, axis=-1))
    west_face = jnp.sqrt(centre * jnp.roll(centre, 1, axis=-1))
    return (north_face, south_face, east_face, west_face)


def relax_colour(padded, forcing, faces, diag_total, ocean_mask, chosen):
    north_face, south_face, east_face, west_face = faces
    middle = padded[:, 1:-1, :]
    pulled = north_face * padded[:, :-2, :] + south_face * padded[:, 2:, :]
    pulled = (
        pulled + east_face * jnp.roll(middle, -1, axis=2) + west_face * jnp.roll(middle, 1, axis=2)
    )
    updated = ocean_mask * (forcing + pulled) / diag_total
    return jnp.where(chosen, updated, middle)


def transform_weights(ssh_cols, obs_column, obs_value, obs_weight, obs_count):
    members, count_blocks, block_span = ssh_cols.shape
    slot_count = obs_column.shape[1]
    float_type = ssh_cols.dtype
    ssh_mean = jnp.mean(ssh_cols, axis=0)
    ssh_pert = ssh_cols - ssh_mean
    picker = (
        obs_column[:, :, None] == jnp.arange(block_span, dtype=jnp.int32)[None, None, :]
    ).astype(float_type)
    seen_pert = jnp.einsum("kbc,bsc->kbs", ssh_pert, picker, precision=precise)
    seen_mean = jnp.einsum("bc,bsc->bs", ssh_mean, picker, precision=precise)
    live_slot = (jnp.arange(slot_count, dtype=jnp.int32)[None, :] < obs_count[:, None]).astype(
        float_type
    )
    obs_scale = live_slot * obs_weight
    obs_info = jnp.einsum("kbs,jbs->bkj", seen_pert * obs_scale[None], seen_pert, precision=precise)
    identity = jnp.eye(members, dtype=float_type)
    system = (members - 1.0) * identity + obs_info
    trace_sum = jnp.trace(system, axis1=1, axis2=2)
    growing = system / trace_sum[:, None, None]
    root_inv = jnp.broadcast_to(identity, growing.shape)
    for step_idx in range(NS_STEPS):
        factor = 1.5 * identity - 0.5 * jnp.matmul(root_inv, growing, precision=precise)
        growing = jnp.matmul(growing, factor, precision=precise)
        root_inv = jnp.matmul(factor, root_inv, precision=precise)
    spread_w = jnp.sqrt((members - 1.0) / trace_sum)[:, None, None] * root_inv
    posterior = jnp.matmul(root_inv, root_inv, precision=precise) / trace_sum[:, None, None]
    innovation = obs_scale * (obs_value - seen_mean)
    pulled = jnp.einsum("kbs,bs->bk", seen_pert, innovation, precision=precise)
    mean_w = jnp.einsum("bjk,bk->bj", posterior, pulled, precision=precise)
    return (ssh_mean, ssh_pert, mean_w[:, :, None] + spread_w)


def apply_surface(ssh_mean, ssh_pert, total_w):
    return ssh_mean[None] + jnp.einsum("jbc,bjk->kbc", ssh_pert, total_w, precision=precise)


def apply_levels(level_cols, total_w):
    level_mean = jnp.mean(level_cols, axis=0)
    level_pert = level_cols - level_mean
    return level_mean[None] + jnp.einsum("jlbc,bjk->klbc", level_pert, total_w, precision=precise)


def local(
    ssh_prior,
    ssh_forcing,
    level_state,
    depth,
    damping,
    land_mask,
    obs_column,
    obs_value,
    obs_weight,
    obs_count,
):
    members, band_rows, grid_cols = ssh_prior.shape
    level_count = level_state.shape[1]
    block_count = band_rows * grid_cols // 128
    level_blocks = level_state.reshape(members, level_count, block_count, 128)
    ocean_mask = land_mask.astype(jnp.float32)
    wet_depth = depth * ocean_mask
    first_row = lax.axis_index("tile") * band_rows
    col_index = jnp.arange(grid_cols, dtype=jnp.int32)[None, :]
    surface = ocean_mask * ssh_prior
    wet_pad = extended(wet_depth, (("tile", 0),), 1)
    faces = face_weights(wet_pad)
    diag_total = damping + faces[0] + faces[1] + faces[2] + faces[3] + (1.0 - ocean_mask)
    parity = (first_row + jnp.arange(band_rows, dtype=jnp.int32)[:, None] + col_index) % 2
    for sweep_idx in range(ITERS):
        for colour in range(2):
            padded = extended(surface, (("tile", 1),), 1)
            surface = relax_colour(
                padded, ssh_forcing, faces, diag_total, ocean_mask, parity == colour
            )
    surface_blocks = surface.reshape(members, 1, block_count, 128)
    local_columns = obs_column[0, 0]
    local_values = obs_value[0, 0]
    local_weights = obs_weight[0, 0]
    local_counts = obs_count[0, 0]
    surface_cols, level_cols = (
        lax.all_to_all(surface_blocks, "mem", split_axis=2, concat_axis=0, tiled=True),
        lax.all_to_all(level_blocks, "mem", split_axis=2, concat_axis=0, tiled=True),
    )
    ssh_mean, ssh_pert, total_w = transform_weights(
        surface_cols[:, 0], local_columns, local_values, local_weights, local_counts
    )
    new_surface = apply_surface(ssh_mean, ssh_pert, total_w)
    new_levels = apply_levels(level_cols, total_w)
    surface_back, levels_back = (
        lax.all_to_all(new_surface[:, None], "mem", split_axis=0, concat_axis=2, tiled=True),
        lax.all_to_all(new_levels, "mem", split_axis=0, concat_axis=2, tiled=True),
    )
    ssh_analysis = surface_back.reshape(members, band_rows, grid_cols)
    level_analysis = levels_back.reshape(members, level_count, band_rows, grid_cols)
    return (ssh_analysis, level_analysis)


def solution(mesh):
    return jax.shard_map(
        local,
        mesh=mesh,
        in_specs=(
            P("mem", "tile", None),
            P("mem", "tile", None),
            P("mem", None, "tile", None),
            P("tile", None),
            P("tile", None),
            P("tile", None),
            P("mem", "tile", None, None),
            P("mem", "tile", None, None),
            P("mem", "tile", None, None),
            P("mem", "tile", None),
        ),
        out_specs=(P("mem", "tile", None), P("mem", None, "tile", None)),
        check_vma=False,
    )
```

profile of v0, /device:TPU:38, one launch (start us, length us, event | category | flops | bytes accessed | tf_op | source)
XLA Modules:
  0.0 465.3 jit_solution(2124864790272536142)
XLA Ops:
  0.6 0.9 convert_multiply_fusion
  1.6 1.9 collective-permute-start
  3.5 3.6 collective-permute-start.2
  7.2 13.1 %collective-permute-start.1 = (f32[2,1,1024]{2,1,0:T(1,128)S(1)}, f32[2,1,1024]{2,1,0:T(1,128)S(1)}, u32[]{:S(2)}, u32[]{:S(2)}) collective-permute-start(f32[2,1,1024]{2,1,0:T(1,128)S(1)} %get-tuple-element.103), channel_id=1, source_target_pairs={{0,1},{1,2},{2,3},{3,4},{4,5},{5,6},{6,7},{7,8},{8,9},{9,10},{10,1... | collective-permute-start | bytes 24584 | tf_op jit(solution)/shard_map/ppermute | solution.py:21
  20.4 1.9 collective-permute-start.3
  23.5 12.0 %collective-permute-done.3 = f32[2,1,1024]{2,1,0:T(1,128)S(1)} collective-permute-done((f32[2,1,1024]{2,1,0:T(1,128)S(1)}, f32[2,1,1024]{2,1,0:T(1,128)S(1)}, u32[]{:S(2)}, u32[]{:S(2)}) %collective-permute-start.3) | collective-permute-done | bytes 8224 | tf_op jit(solution)/shard_map/ppermute | solution.py:23
  35.7 15.1 %collective-permute-start.4 = (f32[2,1,1024]{2,1,0:T(1,128)S(1)}, f32[2,1,1024]{2,1,0:T(1,128)S(1)}, u32[]{:S(2)}, u32[]{:S(2)}) collective-permute-start(f32[2,1,1024]{2,1,0:T(1,128)S(1)} %get-tuple-element.97), channel_id=1, source_target_pairs={{0,1},{1,2},{2,3},{3,4},{4,5},{5,6},{6,7},{7,8},{8,9},{9,10},{10,1... | collective-permute-start | bytes 24584 | tf_op jit(solution)/shard_map/ppermute | solution.py:21
  50.9 1.9 collective-permute-start.5
  52.9 1.3 collective-permute-done.5
  54.4 15.1 %collective-permute-start.6 = (f32[2,1,1024]{2,1,0:T(1,128)S(1)}, f32[2,1,1024]{2,1,0:T(1,128)S(1)}, u32[]{:S(2)}, u32[]{:S(2)}) collective-permute-start(f32[2,1,1024]{2,1,0:T(1,128)S(1)} %get-tuple-element.91), channel_id=1, source_target_pairs={{0,1},{1,2},{2,3},{3,4},{4,5},{5,6},{6,7},{7,8},{8,9},{9,10},{10,1... | collective-permute-start | bytes 24584 | tf_op jit(solution)/shard_map/ppermute | solution.py:21
  69.5 1.9 collective-permute-start.7
  71.5 1.3 collective-permute-done.7
  73.0 14.5 %collective-permute-start.8 = (f32[2,1,1024]{2,1,0:T(1,128)S(1)}, f32[2,1,1024]{2,1,0:T(1,128)S(1)}, u32[]{:S(2)}, u32[]{:S(2)}) collective-permute-start(f32[2,1,1024]{2,1,0:T(1,128)S(1)} %get-tuple-element.85), channel_id=1, source_target_pairs={{0,1},{1,2},{2,3},{3,4},{4,5},{5,6},{6,7},{7,8},{8,9},{9,10},{10,1... | collective-permute-start | bytes 24584 | tf_op jit(solution)/shard_map/ppermute | solution.py:21
  87.4 1.9 collective-permute-start.9
  89.5 1.3 collective-permute-done.9
  91.0 14.5 %collective-permute-start.10 = (f32[2,1,1024]{2,1,0:T(1,128)S(1)}, f32[2,1,1024]{2,1,0:T(1,128)S(1)}, u32[]{:S(2)}, u32[]{:S(2)}) collective-permute-start(f32[2,1,1024]{2,1,0:T(1,128)S(1)} %get-tuple-element.79), channel_id=1, source_target_pairs={{0,1},{1,2},{2,3},{3,4},{4,5},{5,6},{6,7},{7,8},{8,9},{9,10},{10,1... | collective-permute-start | bytes 24584 | tf_op jit(solution)/shard_map/ppermute | solution.py:21
  105.4 1.9 collective-permute-start.11
  107.4 1.3 collective-permute-done.11
  109.0 14.5 %collective-permute-start.12 = (f32[2,1,1024]{2,1,0:T(1,128)S(1)}, f32[2,1,1024]{2,1,0:T(1,128)S(1)}, u32[]{:S(2)}, u32[]{:S(2)}) collective-permute-start(f32[2,1,1024]{2,1,0:T(1,128)S(1)} %get-tuple-element.73), channel_id=1, source_target_pairs={{0,1},{1,2},{2,3},{3,4},{4,5},{5,6},{6,7},{7,8},{8,9},{9,10},{10,1... | collective-permute-start | bytes 24584 | tf_op jit(solution)/shard_map/ppermute | solution.py:21
  123.4 1.9 collective-permute-start.13
  125.4 1.3 collective-permute-done.13
  126.9 14.5 %collective-permute-start.14 = (f32[2,1,1024]{2,1,0:T(1,128)S(1)}, f32[2,1,1024]{2,1,0:T(1,128)S(1)}, u32[]{:S(2)}, u32[]{:S(2)}) collective-permute-start(f32[2,1,1024]{2,1,0:T(1,128)S(1)} %get-tuple-element.67), channel_id=1, source_target_pairs={{0,1},{1,2},{2,3},{3,4},{4,5},{5,6},{6,7},{7,8},{8,9},{9,10},{10,1... | collective-permute-start | bytes 24584 | tf_op jit(solution)/shard_map/ppermute | solution.py:21
  141.4 1.9 collective-permute-start.15
  143.4 1.3 collective-permute-done.15
  144.9 14.5 %collective-permute-start.16 = (f32[2,1,1024]{2,1,0:T(1,128)S(1)}, f32[2,1,1024]{2,1,0:T(1,128)S(1)}, u32[]{:S(2)}, u32[]{:S(2)}) collective-permute-start(f32[2,1,1024]{2,1,0:T(1,128)S(1)} %get-tuple-element.61), channel_id=1, source_target_pairs={{0,1},{1,2},{2,3},{3,4},{4,5},{5,6},{6,7},{7,8},{8,9},{9,10},{10,1... | collective-permute-start | bytes 24584 | tf_op jit(solution)/shard_map/ppermute | solution.py:21
  159.4 1.9 collective-permute-start.17
  161.4 1.3 collective-permute-done.17
  162.9 14.5 %collective-permute-start.18 = (f32[2,1,1024]{2,1,0:T(1,128)S(1)}, f32[2,1,1024]{2,1,0:T(1,128)S(1)}, u32[]{:S(2)}, u32[]{:S(2)}) collective-permute-start(f32[2,1,1024]{2,1,0:T(1,128)S(1)} %get-tuple-element.55), channel_id=1, source_target_pairs={{0,1},{1,2},{2,3},{3,4},{4,5},{5,6},{6,7},{7,8},{8,9},{9,10},{10,1... | collective-permute-start | bytes 24584 | tf_op jit(solution)/shard_map/ppermute | solution.py:21
  177.4 1.9 collective-permute-start.19
  179.4 1.3 collective-permute-done.19
  180.9 14.5 %collective-permute-start.20 = (f32[2,1,1024]{2,1,0:T(1,128)S(1)}, f32[2,1,1024]{2,1,0:T(1,128)S(1)}, u32[]{:S(2)}, u32[]{:S(2)}) collective-permute-start(f32[2,1,1024]{2,1,0:T(1,128)S(1)} %get-tuple-element.49), channel_id=1, source_target_pairs={{0,1},{1,2},{2,3},{3,4},{4,5},{5,6},{6,7},{7,8},{8,9},{9,10},{10,1... | collective-permute-start | bytes 24584 | tf_op jit(solution)/shard_map/ppermute | solution.py:21
  195.4 1.9 collective-permute-start.21
  197.4 1.3 collective-permute-done.21
  198.9 14.5 %collective-permute-start.22 = (f32[2,1,1024]{2,1,0:T(1,128)S(1)}, f32[2,1,1024]{2,1,0:T(1,128)S(1)}, u32[]{:S(2)}, u32[]{:S(2)}) collective-permute-start(f32[2,1,1024]{2,1,0:T(1,128)S(1)} %get-tuple-element.43), channel_id=1, source_target_pairs={{0,1},{1,2},{2,3},{3,4},{4,5},{5,6},{6,7},{7,8},{8,9},{9,10},{10,1... | collective-permute-start | bytes 24584 | tf_op jit(solution)/shard_map/ppermute | solution.py:21
  213.4 1.9 collective-permute-start.23
  215.4 1.3 collective-permute-done.23
  216.9 14.5 %collective-permute-start.24 = (f32[2,1,1024]{2,1,0:T(1,128)S(1)}, f32[2,1,1024]{2,1,0:T(1,128)S(1)}, u32[]{:S(2)}, u32[]{:S(2)}) collective-permute-start(f32[2,1,1024]{2,1,0:T(1,128)S(1)} %get-tuple-element.37), channel_id=1, source_target_pairs={{0,1},{1,2},{2,3},{3,4},{4,5},{5,6},{6,7},{7,8},{8,9},{9,10},{10,1... | collective-permute-start | bytes 24584 | tf_op jit(solution)/shard_map/ppermute | solution.py:21
  231.3 1.9 collective-permute-start.25
  233.4 1.3 collective-permute-done.25
  234.9 14.5 %collective-permute-start.26 = (f32[2,1,1024]{2,1,0:T(1,128)S(1)}, f32[2,1,1024]{2,1,0:T(1,128)S(1)}, u32[]{:S(2)}, u32[]{:S(2)}) collective-permute-start(f32[2,1,1024]{2,1,0:T(1,128)S(1)} %get-tuple-element.31), channel_id=1, source_target_pairs={{0,1},{1,2},{2,3},{3,4},{4,5},{5,6},{6,7},{7,8},{8,9},{9,10},{10,1... | collective-permute-start | bytes 24584 | tf_op jit(solution)/shard_map/ppermute | solution.py:21
  249.3 1.9 collective-permute-start.27
  251.3 1.3 collective-permute-done.27
  252.8 14.5 %collective-permute-start.28 = (f32[2,1,1024]{2,1,0:T(1,128)S(1)}, f32[2,1,1024]{2,1,0:T(1,128)S(1)}, u32[]{:S(2)}, u32[]{:S(2)}) collective-permute-start(f32[2,1,1024]{2,1,0:T(1,128)S(1)} %get-tuple-element.25), channel_id=1, source_target_pairs={{0,1},{1,2},{2,3},{3,4},{4,5},{5,6},{6,7},{7,8},{8,9},{9,10},{10,1... | collective-permute-start | bytes 24584 | tf_op jit(solution)/shard_map/ppermute | solution.py:21
  267.3 1.9 collective-permute-start.29
  269.3 1.3 collective-permute-done.29
  270.8 14.5 %collective-permute-start.30 = (f32[2,1,1024]{2,1,0:T(1,128)S(1)}, f32[2,1,1024]{2,1,0:T(1,128)S(1)}, u32[]{:S(2)}, u32[]{:S(2)}) collective-permute-start(f32[2,1,1024]{2,1,0:T(1,128)S(1)} %get-tuple-element.19), channel_id=1, source_target_pairs={{0,1},{1,2},{2,3},{3,4},{4,5},{5,6},{6,7},{7,8},{8,9},{9,10},{10,1... | collective-permute-start | bytes 24584 | tf_op jit(solution)/shard_map/ppermute | solution.py:21
  285.3 1.9 collective-permute-start.31
  287.3 1.3 collective-permute-done.31
  288.8 14.7 %collective-permute-start.32 = (f32[2,1,1024]{2,1,0:T(1,128)S(1)}, f32[2,1,1024]{2,1,0:T(1,128)S(1)}, u32[]{:S(2)}, u32[]{:S(2)}) collective-permute-start(f32[2,1,1024]{2,1,0:T(1,128)S(1)} %get-tuple-element.13), channel_id=1, source_target_pairs={{0,1},{1,2},{2,3},{3,4},{4,5},{5,6},{6,7},{7,8},{8,9},{9,10},{10,1... | collective-permute-start | bytes 24584 | tf_op jit(solution)/shard_map/ppermute | solution.py:21
  303.5 1.9 collective-permute-start.33
  305.5 1.3 collective-permute-done.33
  307.0 0.8 copy.40
  307.7 8.7 %all-to-all-start = ((f32[2,1,128,128]{3,0,1,2:T(2,128)}), f32[2,1,128,128]{3,0,1,2:T(2,128)S(1)}, u32[]{:S(2)}, u32[]{:S(2)}) async-start(f32[2,1,128,128]{3,0,1,2:T(2,128)} %copy.40), calls=%async_computation | async-start | bytes 262144 | tf_op jit(solution)/shard_map/all_to_all | solution.py:130
  316.6 1.6 copy.45
  318.3 10.3 %all-to-all-done = f32[2,1,128,128]{3,0,1,2:T(2,128)S(1)} async-done(((f32[2,1,128,128]{3,0,1,2:T(2,128)}), f32[2,1,128,128]{3,0,1,2:T(2,128)S(1)}, u32[]{:S(2)}, u32[]{:S(2)}) %all-to-all-start) | async-done | bytes 131104 | tf_op jit(solution)/shard_map/all_to_all | solution.py:130
  328.6 5.7 %all-to-all-start.2 = ((f32[2,8,128,128]{3,1,0,2:T(8,128)}), f32[2,8,128,128]{3,1,0,2:T(8,128)S(1)}, u32[]{:S(2)}, u32[]{:S(2)}) async-start(f32[2,8,128,128]{3,1,0,2:T(8,128)} %copy.45), calls=%async_computation.2 | async-start | bytes 2097152 | tf_op jit(solution)/shard_map/all_to_all | solution.py:131
  345.5 37.7 %all-to-all-done.2 = f32[2,8,128,128]{3,1,0,2:T(8,128)S(1)} async-done(((f32[2,8,128,128]{3,1,0,2:T(8,128)}), f32[2,8,128,128]{3,1,0,2:T(8,128)S(1)}, u32[]{:S(2)}, u32[]{:S(2)}) %all-to-all-start.2) | async-done | bytes 1048608 | tf_op jit(solution)/shard_map/all_to_all | solution.py:131
  383.2 8.1 %all-to-all-start.1 = ((f32[64,1,4,128]{3,2,1,0:T(4,128)}), f32[64,1,4,128]{3,2,1,0:T(4,128)S(1)}, u32[]{:S(2)}, u32[]{:S(2)}) async-start(f32[64,1,4,128]{3,2,1,0:T(4,128)} %copy.43), calls=%async_computation.1 | async-start | bytes 262144 | tf_op jit(solution)/shard_map/all_to_all | solution.py:139
  392.0 1.2 fusion
  393.2 1.6 copy.49
  394.7 10.4 %all-to-all-done.1 = f32[64,1,4,128]{3,2,1,0:T(4,128)S(1)} async-done(((f32[64,1,4,128]{3,2,1,0:T(4,128)}), f32[64,1,4,128]{3,2,1,0:T(4,128)S(1)}, u32[]{:S(2)}, u32[]{:S(2)}) %all-to-all-start.1) | async-done | bytes 131104 | tf_op jit(solution)/shard_map/all_to_all | solution.py:139
  405.1 6.6 %all-to-all-start.3 = ((f32[64,8,4,128]{3,1,2,0:T(8,128)}), f32[64,8,4,128]{3,1,2,0:T(8,128)S(1)}, u32[]{:S(2)}, u32[]{:S(2)}) async-start(f32[64,8,4,128]{3,1,2,0:T(8,128)} %copy.49), calls=%async_computation.3 | async-start | bytes 2097152 | tf_op jit(solution)/shard_map/all_to_all | solution.py:140
  412.4 51.2 %all-to-all-done.3 = f32[64,8,4,128]{3,1,2,0:T(8,128)S(1)} async-done(((f32[64,8,4,128]{3,1,2,0:T(8,128)}), f32[64,8,4,128]{3,1,2,0:T(8,128)S(1)}, u32[]{:S(2)}, u32[]{:S(2)}) %all-to-all-start.3) | async-done | bytes 1048608 | tf_op jit(solution)/shard_map/all_to_all | solution.py:140
  463.9 1.4 reshape.85
  (157 shorter events, 18.7 us)
Async XLA Ops:
  0.6 6.5 %copy-start.2 = (s32[16,1024]{1,0:T(8,128)S(1)}, s32[16,1024]{1,0:T(8,128)}, u32[]{:S(2)}) copy-start(s32[16,1024]{1,0:T(8,128)} %param.15) | copy-start | bytes 196612
  0.6 6.6 %copy-start.3 = (f32[2,16,1024]{2,1,0:T(8,128)S(1)}, f32[2,16,1024]{2,1,0:T(8,128)}, u32[]{:S(2)}) copy-start(f32[2,16,1024]{2,1,0:T(8,128)} %param.10) | copy-start | bytes 393220
  1.6 21.2 %collective-permute-start = (f32[1,1024]{1,0:T(1,128)S(1)}, f32[1,1024]{1,0:T(1,128)S(1)}, u32[]{:S(2)}, u32[]{:S(2)}) collective-permute-start(f32[1,1024]{1,0:T(1,128)S(1)} %get-tuple-element.106), channel_id=1, source_target_pairs={{0,1},{1,2},{2,3},{3,4},{4,5},{5,6},{6,7},{7,8},{8,9},{9,10},{10,1... | collective-permute-start | bytes 12296 | tf_op jit(solution)/shard_map/ppermute | solution.py:21
  3.5 19.3 %collective-permute-start.2 = (f32[1,1024]{1,0:T(1,128)S(1)}, f32[1,1024]{1,0:T(1,128)S(1)}, u32[]{:S(2)}, u32[]{:S(2)}) collective-permute-start(f32[1,1024]{1,0:T(1,128)S(1)} %get-tuple-element.105), channel_id=1, source_target_pairs={{1,0},{2,1},{3,2},{4,3},{5,4},{6,5},{7,6},{8,7},{9,8},{10,9},{11,1... | collective-permute-start | bytes 12296 | tf_op jit(solution)/shard_map/ppermute | solution.py:23
  7.2 16.2 %collective-permute-start.1 = (f32[2,1,1024]{2,1,0:T(1,128)S(1)}, f32[2,1,1024]{2,1,0:T(1,128)S(1)}, u32[]{:S(2)}, u32[]{:S(2)}) collective-permute-start(f32[2,1,1024]{2,1,0:T(1,128)S(1)} %get-tuple-element.103), channel_id=1, source_target_pairs={{0,1},{1,2},{2,3},{3,4},{4,5},{5,6},{6,7},{7,8},{8,9},{9,10},{10,1... | collective-permute-start | bytes 24584 | tf_op jit(solution)/shard_map/ppermute | solution.py:21
  20.4 15.1 %collective-permute-start.3 = (f32[2,1,1024]{2,1,0:T(1,128)S(1)}, f32[2,1,1024]{2,1,0:T(1,128)S(1)}, u32[]{:S(2)}, u32[]{:S(2)}) collective-permute-start(f32[2,1,1024]{2,1,0:T(1,128)S(1)} %get-tuple-element.104), channel_id=1, source_target_pairs={{1,0},{2,1},{3,2},{4,3},{5,4},{6,5},{7,6},{8,7},{9,8},{10,9},{11,1... | collective-permute-start | bytes 24584 | tf_op jit(solution)/shard_map/ppermute | solution.py:23
  22.5 0.8 copy-start.4
  23.3 12.2 %copy-start = (f32[2,16,1024]{2,1,0:T(8,128)S(1)}, f32[2,16,1024]{2,1,0:T(8,128)}, u32[]{:S(2)}) copy-start(f32[2,16,1024]{2,1,0:T(8,128)} %param.11) | copy-start | bytes 393220
  35.7 17.1 %collective-permute-start.4 = (f32[2,1,1024]{2,1,0:T(1,128)S(1)}, f32[2,1,1024]{2,1,0:T(1,128)S(1)}, u32[]{:S(2)}, u32[]{:S(2)}) collective-permute-start(f32[2,1,1024]{2,1,0:T(1,128)S(1)} %get-tuple-element.97), channel_id=1, source_target_pairs={{0,1},{1,2},{2,3},{3,4},{4,5},{5,6},{6,7},{7,8},{8,9},{9,10},{10,1... | collective-permute-start | bytes 24584 | tf_op jit(solution)/shard_map/ppermute | solution.py:21
  50.9 3.3 collective-permute-start.5
  54.4 17.1 %collective-permute-start.6 = (f32[2,1,1024]{2,1,0:T(1,128)S(1)}, f32[2,1,1024]{2,1,0:T(1,128)S(1)}, u32[]{:S(2)}, u32[]{:S(2)}) collective-permute-start(f32[2,1,1024]{2,1,0:T(1,128)S(1)} %get-tuple-element.91), channel_id=1, source_target_pairs={{0,1},{1,2},{2,3},{3,4},{4,5},{5,6},{6,7},{7,8},{8,9},{9,10},{10,1... | collective-permute-start | bytes 24584 | tf_op jit(solution)/shard_map/ppermute | solution.py:21
  69.5 3.3 collective-permute-start.7
  73.0 16.5 %collective-permute-start.8 = (f32[2,1,1024]{2,1,0:T(1,128)S(1)}, f32[2,1,1024]{2,1,0:T(1,128)S(1)}, u32[]{:S(2)}, u32[]{:S(2)}) collective-permute-start(f32[2,1,1024]{2,1,0:T(1,128)S(1)} %get-tuple-element.85), channel_id=1, source_target_pairs={{0,1},{1,2},{2,3},{3,4},{4,5},{5,6},{6,7},{7,8},{8,9},{9,10},{10,1... | collective-permute-start | bytes 24584 | tf_op jit(solution)/shard_map/ppermute | solution.py:21
  87.4 3.3 collective-permute-start.9
  91.0 16.5 %collective-permute-start.10 = (f32[2,1,1024]{2,1,0:T(1,128)S(1)}, f32[2,1,1024]{2,1,0:T(1,128)S(1)}, u32[]{:S(2)}, u32[]{:S(2)}) collective-permute-start(f32[2,1,1024]{2,1,0:T(1,128)S(1)} %get-tuple-element.79), channel_id=1, source_target_pairs={{0,1},{1,2},{2,3},{3,4},{4,5},{5,6},{6,7},{7,8},{8,9},{9,10},{10,1... | collective-permute-start | bytes 24584 | tf_op jit(solution)/shard_map/ppermute | solution.py:21
  105.4 3.3 collective-permute-start.11
  109.0 16.5 %collective-permute-start.12 = (f32[2,1,1024]{2,1,0:T(1,128)S(1)}, f32[2,1,1024]{2,1,0:T(1,128)S(1)}, u32[]{:S(2)}, u32[]{:S(2)}) collective-permute-start(f32[2,1,1024]{2,1,0:T(1,128)S(1)} %get-tuple-element.73), channel_id=1, source_target_pairs={{0,1},{1,2},{2,3},{3,4},{4,5},{5,6},{6,7},{7,8},{8,9},{9,10},{10,1... | collective-permute-start | bytes 24584 | tf_op jit(solution)/shard_map/ppermute | solution.py:21
  123.4 3.3 collective-permute-start.13
  126.9 16.5 %collective-permute-start.14 = (f32[2,1,1024]{2,1,0:T(1,128)S(1)}, f32[2,1,1024]{2,1,0:T(1,128)S(1)}, u32[]{:S(2)}, u32[]{:S(2)}) collective-permute-start(f32[2,1,1024]{2,1,0:T(1,128)S(1)} %get-tuple-element.67), channel_id=1, source_target_pairs={{0,1},{1,2},{2,3},{3,4},{4,5},{5,6},{6,7},{7,8},{8,9},{9,10},{10,1... | collective-permute-start | bytes 24584 | tf_op jit(solution)/shard_map/ppermute | solution.py:21
  141.4 3.3 collective-permute-start.15
  144.9 16.5 %collective-permute-start.16 = (f32[2,1,1024]{2,1,0:T(1,128)S(1)}, f32[2,1,1024]{2,1,0:T(1,128)S(1)}, u32[]{:S(2)}, u32[]{:S(2)}) collective-permute-start(f32[2,1,1024]{2,1,0:T(1,128)S(1)} %get-tuple-element.61), channel_id=1, source_target_pairs={{0,1},{1,2},{2,3},{3,4},{4,5},{5,6},{6,7},{7,8},{8,9},{9,10},{10,1... | collective-permute-start | bytes 24584 | tf_op jit(solution)/shard_map/ppermute | solution.py:21
  159.4 3.3 collective-permute-start.17
  162.9 16.5 %collective-permute-start.18 = (f32[2,1,1024]{2,1,0:T(1,128)S(1)}, f32[2,1,1024]{2,1,0:T(1,128)S(1)}, u32[]{:S(2)}, u32[]{:S(2)}) collective-permute-start(f32[2,1,1024]{2,1,0:T(1,128)S(1)} %get-tuple-element.55), channel_id=1, source_target_pairs={{0,1},{1,2},{2,3},{3,4},{4,5},{5,6},{6,7},{7,8},{8,9},{9,10},{10,1... | collective-permute-start | bytes 24584 | tf_op jit(solution)/shard_map/ppermute | solution.py:21
  177.4 3.3 collective-permute-start.19
  180.9 16.5 %collective-permute-start.20 = (f32[2,1,1024]{2,1,0:T(1,128)S(1)}, f32[2,1,1024]{2,1,0:T(1,128)S(1)}, u32[]{:S(2)}, u32[]{:S(2)}) collective-permute-start(f32[2,1,1024]{2,1,0:T(1,128)S(1)} %get-tuple-element.49), channel_id=1, source_target_pairs={{0,1},{1,2},{2,3},{3,4},{4,5},{5,6},{6,7},{7,8},{8,9},{9,10},{10,1... | collective-permute-start | bytes 24584 | tf_op jit(solution)/shard_map/ppermute | solution.py:21
  195.4 3.3 collective-permute-start.21
  198.9 16.5 %collective-permute-start.22 = (f32[2,1,1024]{2,1,0:T(1,128)S(1)}, f32[2,1,1024]{2,1,0:T(1,128)S(1)}, u32[]{:S(2)}, u32[]{:S(2)}) collective-permute-start(f32[2,1,1024]{2,1,0:T(1,128)S(1)} %get-tuple-element.43), channel_id=1, source_target_pairs={{0,1},{1,2},{2,3},{3,4},{4,5},{5,6},{6,7},{7,8},{8,9},{9,10},{10,1... | collective-permute-start | bytes 24584 | tf_op jit(solution)/shard_map/ppermute | solution.py:21
  213.4 3.3 collective-permute-start.23
  216.9 16.5 %collective-permute-start.24 = (f32[2,1,1024]{2,1,0:T(1,128)S(1)}, f32[2,1,1024]{2,1,0:T(1,128)S(1)}, u32[]{:S(2)}, u32[]{:S(2)}) collective-permute-start(f32[2,1,1024]{2,1,0:T(1,128)S(1)} %get-tuple-element.37), channel_id=1, source_target_pairs={{0,1},{1,2},{2,3},{3,4},{4,5},{5,6},{6,7},{7,8},{8,9},{9,10},{10,1... | collective-permute-start | bytes 24584 | tf_op jit(solution)/shard_map/ppermute | solution.py:21
  231.3 3.3 collective-permute-start.25
  234.9 16.5 %collective-permute-start.26 = (f32[2,1,1024]{2,1,0:T(1,128)S(1)}, f32[2,1,1024]{2,1,0:T(1,128)S(1)}, u32[]{:S(2)}, u32[]{:S(2)}) collective-permute-start(f32[2,1,1024]{2,1,0:T(1,128)S(1)} %get-tuple-element.31), channel_id=1, source_target_pairs={{0,1},{1,2},{2,3},{3,4},{4,5},{5,6},{6,7},{7,8},{8,9},{9,10},{10,1... | collective-permute-start | bytes 24584 | tf_op jit(solution)/shard_map/ppermute | solution.py:21
  249.3 3.3 collective-permute-start.27
  252.8 16.5 %collective-permute-start.28 = (f32[2,1,1024]{2,1,0:T(1,128)S(1)}, f32[2,1,1024]{2,1,0:T(1,128)S(1)}, u32[]{:S(2)}, u32[]{:S(2)}) collective-permute-start(f32[2,1,1024]{2,1,0:T(1,128)S(1)} %get-tuple-element.25), channel_id=1, source_target_pairs={{0,1},{1,2},{2,3},{3,4},{4,5},{5,6},{6,7},{7,8},{8,9},{9,10},{10,1... | collective-permute-start | bytes 24584 | tf_op jit(solution)/shard_map/ppermute | solution.py:21
  267.3 3.3 collective-permute-start.29
  270.8 16.5 %collective-permute-start.30 = (f32[2,1,1024]{2,1,0:T(1,128)S(1)}, f32[2,1,1024]{2,1,0:T(1,128)S(1)}, u32[]{:S(2)}, u32[]{:S(2)}) collective-permute-start(f32[2,1,1024]{2,1,0:T(1,128)S(1)} %get-tuple-element.19), channel_id=1, source_target_pairs={{0,1},{1,2},{2,3},{3,4},{4,5},{5,6},{6,7},{7,8},{8,9},{9,10},{10,1... | collective-permute-start | bytes 24584 | tf_op jit(solution)/shard_map/ppermute | solution.py:21
  285.3 3.3 collective-permute-start.31
  288.8 27.6 %copy-start.1 = (f32[2,8,16,1024]{3,2,1,0:T(8,128)S(1)}, f32[2,8,16,1024]{3,2,1,0:T(8,128)}, u32[]{:S(2)}) copy-start(f32[2,8,16,1024]{3,2,1,0:T(8,128)} %param.12) | copy-start | bytes 3145732
  288.8 16.7 %collective-permute-start.32 = (f32[2,1,1024]{2,1,0:T(1,128)S(1)}, f32[2,1,1024]{2,1,0:T(1,128)S(1)}, u32[]{:S(2)}, u32[]{:S(2)}) collective-permute-start(f32[2,1,1024]{2,1,0:T(1,128)S(1)} %get-tuple-element.13), channel_id=1, source_target_pairs={{0,1},{1,2},{2,3},{3,4},{4,5},{5,6},{6,7},{7,8},{8,9},{9,10},{10,1... | collective-permute-start | bytes 24584 | tf_op jit(solution)/shard_map/ppermute | solution.py:21
  303.5 3.3 collective-permute-start.33
  307.7 20.9 %all-to-all-start = ((f32[2,1,128,128]{3,0,1,2:T(2,128)}), f32[2,1,128,128]{3,0,1,2:T(2,128)S(1)}, u32[]{:S(2)}, u32[]{:S(2)}) async-start(f32[2,1,128,128]{3,0,1,2:T(2,128)} %copy.40), calls=%async_computation | async-start | bytes 262144 | tf_op jit(solution)/shard_map/all_to_all | solution.py:130
  328.6 54.6 %all-to-all-start.2 = ((f32[2,8,128,128]{3,1,0,2:T(8,128)}), f32[2,8,128,128]{3,1,0,2:T(8,128)S(1)}, u32[]{:S(2)}, u32[]{:S(2)}) async-start(f32[2,8,128,128]{3,1,0,2:T(8,128)} %copy.45), calls=%async_computation.2 | async-start | bytes 2097152 | tf_op jit(solution)/shard_map/all_to_all | solution.py:131
  334.5 0.7 copy-start.5
  335.6 0.7 copy-start.7
  335.9 0.7 copy-start.6
  336.0 0.7 copy-start.8
  383.2 21.9 %all-to-all-start.1 = ((f32[64,1,4,128]{3,2,1,0:T(4,128)}), f32[64,1,4,128]{3,2,1,0:T(4,128)S(1)}, u32[]{:S(2)}, u32[]{:S(2)}) async-start(f32[64,1,4,128]{3,2,1,0:T(4,128)} %copy.43), calls=%async_computation.1 | async-start | bytes 262144 | tf_op jit(solution)/shard_map/all_to_all | solution.py:139
  405.1 58.5 %all-to-all-start.3 = ((f32[64,8,4,128]{3,1,2,0:T(8,128)}), f32[64,8,4,128]{3,1,2,0:T(8,128)S(1)}, u32[]{:S(2)}, u32[]{:S(2)}) async-start(f32[64,8,4,128]{3,1,2,0:T(8,128)} %copy.49), calls=%async_computation.3 | async-start | bytes 2097152 | tf_op jit(solution)/shard_map/all_to_all | solution.py:140
where the time goes:
time: 467 us; the launch traced here: 465 us
  starting transfers between devices  297 us (64%)
  waiting for transfers between devices  141 us (30%)
  local copies, waits for them, and re-layouts  12.9 us (3%)
  matrix products  9.75 us (2%)
    ppermute x17, starting transfers between devices, extended(): lax.ppermute(tail, axis, [(i, (i + 1) % count) for i in range(ends)])  234 us
    all_to_all x1, waiting for transfers between devices, local(): lax.all_to_all(new_levels, 'mem', split_axis=0, concat_axis=2, tiled=True)  51.2 us
    all_to_all x1, waiting for transfers between devices, local(): lax.all_to_all(level_blocks, 'mem', split_axis=2, concat_axis=0, tiled=True)  37.7 us
    ppermute x17, starting transfers between devices, extended(): lax.ppermute(head, axis, [((i + 1) % count, i) for i in range(ends)])  34.4 us
    ppermute x17, waiting for transfers between devices, extended(): lax.ppermute(head, axis, [((i + 1) % count, i) for i in range(ends)])  31.1 us
    all_to_all x1, waiting for transfers between devices, local(): lax.all_to_all(new_surface[:, None], 'mem', split_axis=0, concat_axis=2,...  10.4 us
    all_to_all x1, waiting for transfers between devices, local(): lax.all_to_all(surface_blocks, 'mem', split_axis=2, concat_axis=0, tiled=...  10.3 us
  transfers between devices with their start and end apart: 38, of which 20 were waited for; matrix products, arithmetic and copies ran while one was open for 4% of the time, Pallas kernels for 0%

commit v1 on v0

v1 whole, which is shorter than its diff:
```python
import functools

import jax
import jax.numpy as jnp
from jax import lax
from jax.experimental import pallas as pl
from jax.experimental.pallas import tpu as pltpu
from jax.sharding import PartitionSpec as P

ITERS = 8
NS_STEPS = 8
MESH = pl.DeviceIdType.MESH
HI = lax.Precision.HIGHEST
F32 = jnp.float32
BF16 = jnp.bfloat16

PB, FR, FB, WR, WB, DR, DB, HALO = 0, 16, 32, 48, 56, 64, 72, 80
FIRST = 4


def split(x):
    high = x.astype(BF16)
    return high, (x - high.astype(F32)).astype(BF16)


def dot(a, b, dims=(((1,), (0,)), ((), ())), precision=None):
    return lax.dot_general(a, b, dims, precision=precision, preferred_element_type=F32)


NT = (((1,), (1,)), ((), ()))


def kernel(
    mems, tiles, prior, forcing, levels, depth, damping, mask, ocol, oval, owgt, ocnt, outs, outl,
    halo, ls, lr, ss, sr, back, rb, vr, vb, swr, swb, coef, halo_send, halo_recv, send, recv,
):
    me = lax.axis_index("mem")
    band = lax.axis_index("tile")
    has_north, has_south = band > 0, band < tiles - 1

    barrier = pltpu.get_barrier_semaphore()

    def greet(i, carry):
        pl.semaphore_signal(barrier, inc=1, device_id={"mem": lax.rem(me + i, mems)}, device_id_type=MESH)
        return carry

    @pl.when(has_north)
    def _():
        pl.semaphore_signal(barrier, inc=1, device_id={"tile": band - 1}, device_id_type=MESH)

    @pl.when(has_south)
    def _():
        pl.semaphore_signal(barrier, inc=1, device_id={"tile": band + 1}, device_id_type=MESH)

    lax.fori_loop(1, mems, greet, 0)

    lane = lax.broadcasted_iota(jnp.int32, (8, 128), 1)
    sub = lax.broadcasted_iota(jnp.int32, (8, 128), 0)
    even = (lane % 2 == 0)[None]
    first_lane = (lane == 0)[None]
    last_lane = (lane == 127)[None]
    low_half = (sub < 4)[None]

    def rows_first(x):
        parts = []
        for octet in range(2):
            cut = [x[8 * octet : 8 * octet + 8, 128 * b : 128 * b + 128] for b in range(8)]
            parts.append(jnp.swapaxes(jnp.stack(cut, axis=0), 0, 1))
        return jnp.concatenate(parts, axis=0)

    def colours(x):
        x = rows_first(x).reshape(8, 2, 8, 128)
        top, bottom = x[:, 0], x[:, 1]
        return jnp.where(even, top, bottom), jnp.where(even, bottom, top)

    wet_red, wet_black = colours(depth[...] * mask[...].astype(F32))
    halo[1, WR : WR + 8] = wet_red
    halo[1, WB : WB + 8] = wet_black
    damp_red, damp_black = colours(damping[...])
    halo[1, DR : DR + 8] = damp_red
    halo[1, DB : DB + 8] = damp_black
    for a in range(2):
        halo[1, PB + 8 * a : PB + 8 * a + 8] = colours(prior[a])[1]
        red, black = colours(forcing[a])
        halo[1, FR + 8 * a : FR + 8 * a + 8] = red
        halo[1, FB + 8 * a : FB + 8 * a + 8] = black

    @pl.when(jnp.logical_not(has_north))
    def _():
        halo[0] = jnp.zeros((HALO, 8, 128), F32)

    @pl.when(jnp.logical_not(has_south))
    def _():
        halo[2] = jnp.zeros((HALO, 8, 128), F32)

    pl.semaphore_wait(barrier, mems - 1 + has_north.astype(jnp.int32) + has_south.astype(jnp.int32))

    to_south = pltpu.make_async_remote_copy(
        src_ref=halo.at[1], dst_ref=halo.at[0], send_sem=halo_send.at[0], recv_sem=halo_recv.at[0],
        device_id={"tile": jnp.minimum(band + 1, tiles - 1)}, device_id_type=MESH,
    )
    to_north = pltpu.make_async_remote_copy(
        src_ref=halo.at[1], dst_ref=halo.at[2], send_sem=halo_send.at[1], recv_sem=halo_recv.at[1],
        device_id={"tile": jnp.maximum(band - 1, 0)}, device_id_type=MESH,
    )

    @pl.when(has_south)
    def _():
        to_south.start()

    @pl.when(has_north)
    def _():
        to_north.start()

    for octet in range(2):
        for b in range(8):
            for a in range(2):
                cut = levels[a, :, 8 * octet : 8 * octet + 8, 128 * b : 128 * b + 128]
                ls[8 * octet : 8 * octet + 8, b // 4, 2 * (b % 4) + a] = jnp.swapaxes(cut, 0, 1)

    def scatter(src_of, dst, which):
        def one(i, carry):
            peer = lax.rem(me + i, mems)
            pltpu.make_async_remote_copy(
                src_ref=src_of(peer), dst_ref=dst, send_sem=send.at[which], recv_sem=recv.at[which],
                device_id={"mem": peer}, device_id_type=MESH,
            ).start()
            return carry

        lax.fori_loop(1, mems, one, 0)

    def finish(ref, sem):
        pltpu.make_async_copy(ref, ref, sem).wait()

    scatter(lambda p: ls.at[p // 2, p % 2, pl.ds(0, FIRST)], lr.at[me, pl.ds(0, FIRST)], 0)
    lr[me] = ls[me // 2, me % 2]

    @pl.when(has_north)
    def _():
        to_south.wait_recv()

    @pl.when(has_south)
    def _():
        to_north.wait_recv()

    def stacked(index):
        return jnp.concatenate([halo[0, index : index + 8], halo[1, index : index + 8], halo[2, index : index + 8]], axis=0)

    zero = jnp.zeros((8, 128), F32)
    for ref in (swr, swb):
        ref[0] = zero
        ref[25] = zero
    for ref in (vr, vb):
        for a in range(2):
            ref[a, 0] = zero
            ref[a, 25] = zero
    swr[1:25] = jnp.sqrt(stacked(WR))
    swb[1:25] = jnp.sqrt(stacked(WB))

    def east(x):
        y = pltpu.roll(x, 127, 2)
        return jnp.where(last_lane, pltpu.roll(y, 7, 1), y)

    def west(x):
        y = pltpu.roll(x, 1, 2)
        return jnp.where(first_lane, pltpu.roll(y, 1, 1), y)

    def around(ref, at, red, lead=()):
        x = ref[lead + (slice(at, at + 8),)]
        up = ref[lead + (slice(at - 1, at + 7),)]
        down = ref[lead + (slice(at + 1, at + 9),)]
        other = jnp.where(even, up, down) if red else jnp.where(even, down, up)
        return (x + other) + (east(x) + west(x))

    for part in range(3):
        at = 1 + 8 * part
        for red in (True, False):
            own, other = (swr, swb) if red else (swb, swr)
            root = own[at : at + 8]
            wet = halo[part, (WR if red else WB) : (WR if red else WB) + 8]
            damp = halo[part, (DR if red else DB) : (DR if red else DB) + 8]
            diag = damp + root * around(other, at, red) + jnp.where(wet > 0, 0.0, 1.0)
            inverse = 1.0 / diag
            col = 0 if red else 1
            coef[col, at : at + 8] = wet * inverse
            gain = root * inverse
            for a in range(2):
                start = (FR if red else FB) + 8 * a
                coef[2 + 2 * a + col, at : at + 8] = gain * halo[part, start : start + 8]
                if not red:
                    vb[a, at : at + 8] = root * halo[part, PB + 8 * a : PB + 8 * a + 8]

    def sweep(_, carry):
        for red in (True, False):
            own, other = (vr, vb) if red else (vb, vr)
            col = 0 if red else 1
            for a in range(2):
                for part in range(3):
                    at = 1 + 8 * part
                    own[a, at : at + 8] = coef[2 + 2 * a + col, at : at + 8] + coef[col, at : at + 8] * around(
                        other, at, red, (a,)
                    )
        return carry

    lax.fori_loop(0, ITERS, sweep, 0)

    inv_red = jnp.where(wet_red > 0, 1.0 / swr[9:17], 0.0)
    inv_black = jnp.where(wet_black > 0, 1.0 / swb[9:17], 0.0)
    rows = []
    for a in range(2):
        red, black = vr[a, 9:17] * inv_red, vb[a, 9:17] * inv_black
        rows.append((jnp.where(even, red, black), jnp.where(even, black, red)))
    halves = []
    for par in range(2):
        x0, x1 = rows[0][par], rows[1][par]
        halves.append(jnp.where(low_half, x0, pltpu.roll(x1, 4, 1)))
        halves.append(jnp.where(low_half, pltpu.roll(x0, 4, 1), x1))
    ss[...] = jnp.stack(halves, axis=1).reshape(mems, 8, 128)
    scatter(lambda p: ss.at[p], sr.at[me], 1)
    scatter(lambda p: ls.at[p // 2, p % 2, pl.ds(FIRST, 8 - FIRST)], lr.at[me, pl.ds(FIRST, 8 - FIRST)], 2)
    sr[me] = ss[me]

    @pl.when(has_south)
    def _():
        to_south.wait_send()

    @pl.when(has_north)
    def _():
        to_north.wait_send()

    members = 2 * mems
    finish(sr.at[pl.ds(0, mems - 1)], recv.at[1])
    seen_all = jnp.swapaxes(sr[...], 0, 1)
    eye = (
        lax.broadcasted_iota(jnp.int32, (members, members), 0) == lax.broadcasted_iota(jnp.int32, (members, members), 1)
    ).astype(F32)
    cells = lax.broadcasted_iota(jnp.int32, (128, 128), 0)
    slot = lax.broadcasted_iota(jnp.int32, (1, 128), 1)
    surf, grow, drive, traces = [], [], [], []
    for j in range(4):
        s = jnp.concatenate([seen_all[j], seen_all[4 + j]], axis=0)
        surf.append(s)
        pick = (cells == ocol[j : j + 1, :]).astype(F32).astype(BF16)
        high, low = split(s)
        seen = dot(high, pick) + dot(low, pick)
        mean = jnp.mean(seen, axis=0, keepdims=True)
        pert = seen - mean
        scale = jnp.where(slot < ocnt[j], owgt[j : j + 1, :], 0.0)
        innov = scale * (oval[j : j + 1, :] - mean)
        system = (members - 1.0) * eye + dot(pert * scale, pert, NT, HI)
        trace = jnp.sum(jnp.sum(system * eye, axis=1, keepdims=True), axis=0, keepdims=True)
        traces.append(trace)
        grow.append(system / trace)
        drive.append(dot(jnp.broadcast_to(innov, (8, 128)), pert, NT, HI)[0:1])

    def iterate(_, carry):
        out = []
        for j in range(4):
            g, r = carry[2 * j], carry[2 * j + 1]
            f = 1.5 * eye - 0.5 * dot(r, g, precision=HI)
            out += [dot(g, f, precision=HI), dot(f, r, precision=HI)]
        return tuple(out)

    state = []
    for j in range(4):
        state += [grow[j], eye]
    for _ in range(NS_STEPS): state = iterate(0, state)

    finish(lr.at[pl.ds(0, mems - 1), pl.ds(0, FIRST)], recv.at[0])
    finish(lr.at[pl.ds(0, mems - 1), pl.ds(FIRST, 8 - FIRST)], recv.at[2])
    tail = []
    for j in range(4):
        root = state[2 * j + 1]
        inner = jnp.sum(root * drive[j], axis=1, keepdims=True)
        mean_w = jnp.sum(root * inner, axis=0, keepdims=True) / traces[j]
        w = mean_w + jnp.sqrt((members - 1.0) / traces[j]) * root
        w = w - jnp.mean(w, axis=1, keepdims=True) + 1.0 / members
        w_high, w_low = split(w)
        turned = [jnp.swapaxes(lr[:, 2 * j + a], 0, 1) for a in range(2)]
        x = jnp.concatenate([jnp.concatenate([turned[0][l], turned[1][l]], axis=0) for l in range(8)] + [surf[j]], axis=1)
        x_high, x_low = split(x)
        y = dot(w_high, x_high) + (dot(w_high, x_low) + dot(w_low, x_high))
        for a in range(2):
            piece = jnp.stack([y[mems * a : mems * a + mems, 128 * l : 128 * l + 128] for l in range(8)], axis=0)
            back[:, 2 * j + a] = jnp.swapaxes(piece, 0, 1)
        tail.append([y[0:mems, 1024:1152], y[mems:members, 1024:1152]])
    flat = jnp.stack([tail[j][a] for a in range(2) for j in range(4)], axis=0)
    back[:, 8] = jnp.swapaxes(flat, 0, 1)
    scatter(lambda p: back.at[p], rb.at[me // 2, me % 2], 3)
    rb[me // 2, me % 2] = back[me]

    finish(ls.at[pl.ds(0, 15), :, pl.ds(0, FIRST)], send.at[0])
    finish(ls.at[0, 0, pl.ds(0, FIRST)], send.at[0])
    finish(ss.at[pl.ds(0, mems - 1)], send.at[1])
    finish(ls.at[pl.ds(0, 15), :, pl.ds(FIRST, 8 - FIRST)], send.at[2])
    finish(ls.at[0, 0, pl.ds(FIRST, 8 - FIRST)], send.at[2])
    finish(back.at[pl.ds(0, mems - 1)], recv.at[3])
    for octet in range(2):
        for h in range(2):
            for j in range(4):
                left = 128 * (4 * h + j)
                for a in range(2):
                    x = jnp.swapaxes(rb[8 * octet : 8 * octet + 8, h, 2 * j + a], 0, 1)
                    outl[a, :, 8 * octet : 8 * octet + 8, left : left + 128] = x
            x = jnp.swapaxes(rb[8 * octet : 8 * octet + 8, h, 8], 0, 1)
            for j in range(4):
                left = 128 * (4 * h + j)
                for a in range(2):
                    outs[a, 8 * octet : 8 * octet + 8, left : left + 128] = x[4 * a + j]
    finish(back.at[pl.ds(0, mems - 1)], send.at[3])


def local(
    ssh_prior, ssh_forcing, level_state, depth, damping, land_mask, obs_column, obs_value, obs_weight, obs_count
):
    mems, tiles = lax.axis_size("mem"), lax.axis_size("tile")
    vmem = pl.BlockSpec(memory_space=pltpu.VMEM)
    return pl.pallas_call(
        functools.partial(kernel, mems, tiles),
        out_shape=(
            jax.ShapeDtypeStruct(ssh_prior.shape, F32),
            jax.ShapeDtypeStruct(level_state.shape, F32),
        ),
        in_specs=[vmem] * 9 + [pl.BlockSpec(memory_space=pltpu.SMEM)],
        out_specs=(vmem, vmem),
        scratch_shapes=[
            pltpu.VMEM((3, HALO, 8, 128), F32),
            pltpu.VMEM((16, 2, 8, 8, 128), F32),
            pltpu.VMEM((mems, 8, 8, 128), F32),
            pltpu.VMEM((mems, 8, 128), F32),
            pltpu.VMEM((mems, 8, 128), F32),
            pltpu.VMEM((mems, 9, 8, 128), F32),
            pltpu.VMEM((16, 2, 9, 8, 128), F32),
            pltpu.VMEM((2, 26, 8, 128), F32),
            pltpu.VMEM((2, 26, 8, 128), F32),
            pltpu.VMEM((26, 8, 128), F32),
            pltpu.VMEM((26, 8, 128), F32),
            pltpu.VMEM((6, 26, 8, 128), F32),
            pltpu.SemaphoreType.DMA((2,)),
            pltpu.SemaphoreType.DMA((2,)),
            pltpu.SemaphoreType.DMA((4,)),
            pltpu.SemaphoreType.DMA((4,)),
        ],
        compiler_params=pltpu.CompilerParams(collective_id=0, has_side_effects=True),
        name="relax_letkf",
    )(
        ssh_prior, ssh_forcing, level_state, depth, damping, land_mask,
        obs_column[0, 0], obs_value[0, 0], obs_weight[0, 0], obs_count[0, 0],
    )


def solution(mesh):
    return jax.shard_map(
        local,
        mesh=mesh,
        in_specs=(
            P("mem", "tile", None),
            P("mem", "tile", None),
            P("mem", None, "tile", None),
            P("tile", None),
            P("tile", None),
            P("tile", None),
            P("mem", "tile", None, None),
            P("mem", "tile", None, None),
            P("mem", "tile", None, None),
            P("mem", "tile", None),
        ),
        out_specs=(P("mem", "tile", None), P("mem", None, "tile", None)),
        check_vma=False,
    )
```

time: 467 us -> 132 us (0.28)
  the two profiles are of different devices: /device:TPU:38 before, /device:TPU:24 now
where the time goes in v1:
time: 132 us
  Pallas kernels  128 us (97%)
  local copies, waits for them, and re-layouts  3.87 us (3%)
    pallas_call x1, Pallas kernels, local(): pl.pallas_call(functools.partial(kernel, mems, tiles), out_shape=(jax.Sha...  128 us
    unnamed x2, local copies, waits for them, and re-layouts  3.87 us

profile of v1, /device:TPU:24, one launch (start us, length us, event | category | flops | bytes accessed | tf_op | source)
XLA Modules:
  0.0 132.1 jit_solution(11444601513956031500)
XLA Ops:
  0.6 127.6 %relax_letkf.1 = (f32[2,16,1024]{2,1,0:T(8,128)}, f32[2,8,16,1024]{3,2,1,0:T(8,128)}) custom-call(f32[2,16,1024]{2,1,0:T(8,128)} %prior.1, f32[2,16,1024]{2,1,0:T(8,128)} %forcing.1, f32[2,8,16,1024]{3,2,1,0:T(8,128)} %levels.1, f32[16,1024]{1,0:T(8,128)} %depth.1, f32[16,1024]{1,0:T(8,128)} %damping.1, s32[16,1024]{1,0:T(8,128)} %mask.1, s32[4,128]{1,0:T(4,128)} %bitcast.4, ...), custom_call_target="tpu_custom_call" | custom-call | tf_op jit(solution)/shard_map/relax_letkf/pallas_call | solution.py:318
  128.2 1.6 %copy.14 = f32[2,16,1024]{2,1,0:T(8,128)} copy(f32[2,16,1024]{2,1,0:T(8,128)} %get-tuple-element.4) | data formatting | bytes 262144
  129.8 2.3 %copy.15 = f32[2,8,16,1024]{3,2,1,0:T(8,128)} copy(f32[2,8,16,1024]{3,2,1,0:T(8,128)} %get-tuple-element.5) | data formatting | bytes 2097152

commit v2 on v1

--- a/solution.py
+++ b/solution.py
@@ -15,6 +15,8 @@
 BF16 = jnp.bfloat16
 
 PB, FR, FB, WR, WB, DR, DB, HALO = 0, 16, 32, 48, 56, 64, 72, 80
+QUARTER = HALO // 4
+FAR = 8
 FIRST = 4
 
 
@@ -31,12 +33,19 @@
 
 
 def kernel(
-    mems, tiles, prior, forcing, levels, depth, damping, mask, ocol, oval, owgt, ocnt, outs, outl,
-    halo, ls, lr, ss, sr, back, rb, vr, vb, swr, swb, coef, halo_send, halo_recv, send, recv,
+    mems, tiles, prior_hbm, forcing_hbm, levels_hbm, depth_hbm, damping_hbm, mask_hbm, ocol_hbm, oval_hbm, owgt_hbm, ocnt_hbm, rb,
+    prior, forcing, levels, depth, damping, mask, ocol, oval, owgt, ocnt,
+    halo, relay, ls, lr, ss, sr, back, vr, vb, swr, swb, coef,
+    halo_send, halo_recv, relay_send, relay_recv, send, recv, fetch,
 ):
     me = lax.axis_index("mem")
     band = lax.axis_index("tile")
+    above, below = band == FAR - 1, band == FAR
+    low = (band == 0) | (band == 2) | (band == 4)
+    high = (band == FAR + 2) | (band == FAR + 4) | (band == FAR + 7)
+    quarter = pl.ds(lax.rem(band, FAR) // 2 * QUARTER, QUARTER)
     has_north, has_south = band > 0, band < tiles - 1
+    near_north, near_south = has_north & jnp.logical_not(below), has_south & jnp.logical_not(above)
 
     barrier = pltpu.get_barrier_semaphore()
 
@@ -44,15 +53,33 @@
         pl.semaphore_signal(barrier, inc=1, device_id={"mem": lax.rem(me + i, mems)}, device_id_type=MESH)
         return carry
 
-    @pl.when(has_north)
-    def _():
-        pl.semaphore_signal(barrier, inc=1, device_id={"tile": band - 1}, device_id_type=MESH)
-
-    @pl.when(has_south)
-    def _():
-        pl.semaphore_signal(barrier, inc=1, device_id={"tile": band + 1}, device_id_type=MESH)
+    def hail(role, *targets):
+        @pl.when(role)
+        def _():
+            for target in targets:
+                pl.semaphore_signal(barrier, inc=1, device_id={"tile": target}, device_id_type=MESH)
 
     lax.fori_loop(1, mems, greet, 0)
+    hail(near_north, band - 1)
+    hail(near_south, band + 1)
+    hail(above, 0, 2, 4, FAR + 7)
+    hail(below, 0, FAR + 2, FAR + 4, FAR + 7)
+    hail(low, FAR - 1, band + FAR)
+    hail(high, FAR, band - FAR)
+    greetings = mems - 1 + near_north.astype(jnp.int32) + near_south.astype(jnp.int32)
+    greetings += 4 * (above | below).astype(jnp.int32) + 2 * (low | high).astype(jnp.int32)
+
+    fetches = [
+        pltpu.make_async_copy(src, dst, fetch.at[n])
+        for n, (src, dst) in enumerate((
+            (depth_hbm, depth), (mask_hbm, mask), (damping_hbm, damping), (prior_hbm, prior), (forcing_hbm, forcing),
+            (levels_hbm, levels), (ocol_hbm, ocol), (oval_hbm, oval), (owgt_hbm, owgt), (ocnt_hbm, ocnt),
+        ))
+    ]
+    for copy in fetches:
+        copy.start()
+    for copy in fetches[:5]:
+        copy.wait()
 
     lane = lax.broadcasted_iota(jnp.int32, (8, 128), 1)
     sub = lax.broadcasted_iota(jnp.int32, (8, 128), 0)
@@ -93,30 +120,58 @@
     def _():
         halo[2] = jnp.zeros((HALO, 8, 128), F32)
 
-    pl.semaphore_wait(barrier, mems - 1 + has_north.astype(jnp.int32) + has_south.astype(jnp.int32))
-
-    to_south = pltpu.make_async_remote_copy(
-        src_ref=halo.at[1], dst_ref=halo.at[0], send_sem=halo_send.at[0], recv_sem=halo_recv.at[0],
-        device_id={"tile": jnp.minimum(band + 1, tiles - 1)}, device_id_type=MESH,
-    )
-    to_north = pltpu.make_async_remote_copy(
-        src_ref=halo.at[1], dst_ref=halo.at[2], send_sem=halo_send.at[1], recv_sem=halo_recv.at[1],
-        device_id={"tile": jnp.maximum(band - 1, 0)}, device_id_type=MESH,
-    )
-
-    @pl.when(has_south)
-    def _():
-        to_south.start()
-
-    @pl.when(has_north)
-    def _():
-        to_north.start()
-
+    fetches[5].wait()
     for octet in range(2):
         for b in range(8):
             for a in range(2):
                 cut = levels[a, :, 8 * octet : 8 * octet + 8, 128 * b : 128 * b + 128]
                 ls[8 * octet : 8 * octet + 8, b // 4, 2 * (b % 4) + a] = jnp.swapaxes(cut, 0, 1)
+
+    pl.semaphore_wait(barrier, greetings)
+
+    to_south = pltpu.make_async_remote_copy(
+        src_ref=halo.at[1], dst_ref=halo.at[0], send_sem=halo_send.at[0], recv_sem=halo_recv.at[0],
+        device_id={"tile": lax.rem(band + 1, tiles)}, device_id_type=MESH,
+    )
+    to_north = pltpu.make_async_remote_copy(
+        src_ref=halo.at[1], dst_ref=halo.at[2], send_sem=halo_send.at[1], recv_sem=halo_recv.at[1],
+        device_id={"tile": lax.rem(band + tiles - 1, tiles)}, device_id_type=MESH,
+    )
+
+    @pl.when(near_south)
+    def _():
+        to_south.start()
+
+    @pl.when(near_north)
+    def _():
+        to_north.start()
+
+    def hand(src, dst, send_sem, recv_sem, target):
+        return pltpu.make_async_remote_copy(
+            src_ref=src, dst_ref=dst, send_sem=send_sem, recv_sem=recv_sem, device_id={"tile": target}, device_id_type=MESH
+        )
+
+    @pl.when(above)
+    def _():
+        for q, target in enumerate((0, 2, 4, FAR + 7)):
+            hand(halo.at[1, pl.ds(q * QUARTER, QUARTER)], relay.at[0], halo_send.at[0], relay_recv.at[0], target).start()
+
+    @pl.when(below)
+    def _():
+        for q, target in enumerate((0, FAR + 2, FAR + 4, FAR + 7)):
+            hand(halo.at[1, pl.ds(q * QUARTER, QUARTER)], relay.at[1], halo_send.at[1], relay_recv.at[1], target).start()
+
+    def pass_on(role, way, dst, recv_sem, target):
+        @pl.when(role)
+        def _():
+            copy = hand(relay.at[way], dst, relay_send.at[way], recv_sem, target)
+            pltpu.make_async_copy(relay.at[way], relay.at[way], relay_recv.at[way]).wait()
+            copy.start()
+
+    pass_on(band == 0, 0, halo.at[0, quarter], halo_recv.at[0], FAR)
+    pass_on((band == 2) | (band == 4), 0, relay.at[0], relay_recv.at[0], lax.rem(band + FAR, tiles))
+    pass_on(band == FAR + 7, 1, halo.at[2, quarter], halo_recv.at[1], FAR - 1)
+    pass_on((band == FAR + 2) | (band == FAR + 4), 1, relay.at[1], relay_recv.at[1], lax.rem(band + FAR, tiles))
 
     def scatter(src_of, dst, which):
         def one(i, carry):
@@ -134,6 +189,9 @@
 
     scatter(lambda p: ls.at[p // 2, p % 2, pl.ds(0, FIRST)], lr.at[me, pl.ds(0, FIRST)], 0)
     lr[me] = ls[me // 2, me % 2]
+
+    pass_on(high, 0, halo.at[0, quarter], halo_recv.at[0], FAR)
+    pass_on(low, 1, halo.at[2, quarter], halo_recv.at[1], FAR - 1)
 
     @pl.when(has_north)
     def _():
@@ -227,6 +285,14 @@
     @pl.when(has_north)
     def _():
         to_north.wait_send()
+
+    @pl.when(low | high)
+    def _():
+        for way in range(2):
+            pltpu.make_async_copy(relay.at[way], relay.at[way], relay_send.at[way]).wait()
+
+    for copy in fetches[6:]:
+        copy.wait()
 
     members = 2 * mems
     finish(sr.at[pl.ds(0, mems - 1)], recv.at[1])
@@ -266,10 +332,18 @@
         state += [grow[j], eye]
     for _ in range(NS_STEPS): state = iterate(0, state)
 
-    finish(lr.at[pl.ds(0, mems - 1), pl.ds(0, FIRST)], recv.at[0])
-    finish(lr.at[pl.ds(0, mems - 1), pl.ds(FIRST, 8 - FIRST)], recv.at[2])
     tail = []
+    def give(first, count, which):
+        part = pl.ds(first, count)
+        scatter(lambda p: back.at[p, part], rb.at[me // 2, me % 2, part], which)
+        pltpu.make_async_copy(back.at[me, part], rb.at[me // 2, me % 2, part], fetch.at[which]).start()
+
     for j in range(4):
+        if j == 0:
+            finish(lr.at[pl.ds(0, mems - 1), pl.ds(0, FIRST)], recv.at[0])
+        if 2 * j == FIRST:
+            give(0, FIRST, 3)
+            finish(lr.at[pl.ds(0, mems - 1), pl.ds(FIRST, 8 - FIRST)], recv.at[2])
         root = state[2 * j + 1]
         inner = jnp.sum(root * drive[j], axis=1, keepdims=True)
         mean_w = jnp.sum(root * inner, axis=0, keepdims=True) / traces[j]
@@ -286,51 +360,53 @@
         tail.append([y[0:mems, 1024:1152], y[mems:members, 1024:1152]])
     flat = jnp.stack([tail[j][a] for a in range(2) for j in range(4)], axis=0)
     back[:, 8] = jnp.swapaxes(flat, 0, 1)
-    scatter(lambda p: back.at[p], rb.at[me // 2, me % 2], 3)
-    rb[me // 2, me % 2] = back[me]
+    give(FIRST, 9 - FIRST, 4)
 
     finish(ls.at[pl.ds(0, 15), :, pl.ds(0, FIRST)], send.at[0])
     finish(ls.at[0, 0, pl.ds(0, FIRST)], send.at[0])
     finish(ss.at[pl.ds(0, mems - 1)], send.at[1])
     finish(ls.at[pl.ds(0, 15), :, pl.ds(FIRST, 8 - FIRST)], send.at[2])
     finish(ls.at[0, 0, pl.ds(FIRST, 8 - FIRST)], send.at[2])
-    finish(back.at[pl.ds(0, mems - 1)], recv.at[3])
-    for octet in range(2):
-        for h in range(2):
-            for j in range(4):
-                left = 128 * (4 * h + j)
-                for a in range(2):
-                    x = jnp.swapaxes(rb[8 * octet : 8 * octet + 8, h, 2 * j + a], 0, 1)
-                    outl[a, :, 8 * octet : 8 * octet + 8, left : left + 128] = x
-            x = jnp.swapaxes(rb[8 * octet : 8 * octet + 8, h, 8], 0, 1)
-            for j in range(4):
-                left = 128 * (4 * h + j)
-                for a in range(2):
-                    outs[a, 8 * octet : 8 * octet + 8, left : left + 128] = x[4 * a + j]
-    finish(back.at[pl.ds(0, mems - 1)], send.at[3])
+    for which, part in ((3, pl.ds(0, FIRST)), (4, pl.ds(FIRST, 9 - FIRST))):
+        pltpu.make_async_copy(back.at[me, part], rb.at[me // 2, me % 2, part], fetch.at[which]).wait()
+        finish(back.at[pl.ds(0, mems - 1), part], send.at[which])
+        finish(back.at[pl.ds(0, mems - 1), part], recv.at[which])
+
+
+def arrange(rb, outs, outl):
+    for j in range(4):
+        for a in range(2):
+            outl[a, :, :, 128 * j : 128 * j + 128] = jnp.swapaxes(rb[:, 0, 2 * j + a], 0, 1)
+    x = jnp.swapaxes(rb[:, 0, 8], 0, 1)
+    for j in range(4):
+        for a in range(2):
+            outs[a, :, 128 * j : 128 * j + 128] = x[4 * a + j]
 
 
 def local(
     ssh_prior, ssh_forcing, level_state, depth, damping, land_mask, obs_column, obs_value, obs_weight, obs_count
 ):
     mems, tiles = lax.axis_size("mem"), lax.axis_size("tile")
-    vmem = pl.BlockSpec(memory_space=pltpu.VMEM)
-    return pl.pallas_call(
+    operands = (
+        ssh_prior, ssh_forcing, level_state, depth, damping, land_mask,
+        obs_column[0, 0], obs_value[0, 0], obs_weight[0, 0], obs_count[0, 0],
+    )
+    anywhere = pl.BlockSpec(memory_space=pl.ANY)
+    landed = pl.pallas_call(
         functools.partial(kernel, mems, tiles),
-        out_shape=(
-            jax.ShapeDtypeStruct(ssh_prior.shape, F32),
-            jax.ShapeDtypeStruct(level_state.shape, F32),
-        ),
-        in_specs=[vmem] * 9 + [pl.BlockSpec(memory_space=pltpu.SMEM)],
-        out_specs=(vmem, vmem),
+        out_shape=jax.ShapeDtypeStruct((16, 2, 9, 8, 128), F32),
+        in_specs=[anywhere] * 10,
+        out_specs=anywhere,
         scratch_shapes=[
+            *(pltpu.VMEM(x.shape, x.dtype) for x in operands[:9]),
+            pltpu.SMEM(operands[9].shape, operands[9].dtype),
             pltpu.VMEM((3, HALO, 8, 128), F32),
+            pltpu.VMEM((2, QUARTER, 8, 128), F32),
             pltpu.VMEM((16, 2, 8, 8, 128), F32),
             pltpu.VMEM((mems, 8, 8, 128), F32),
             pltpu.VMEM((mems, 8, 128), F32),
             pltpu.VMEM((mems, 8, 128), F32),
             pltpu.VMEM((mems, 9, 8, 128), F32),
-            pltpu.VMEM((16, 2, 9, 8, 128), F32),
             pltpu.VMEM((2, 26, 8, 128), F32),
             pltpu.VMEM((2, 26, 8, 128), F32),
             pltpu.VMEM((26, 8, 128), F32),
@@ -338,15 +414,29 @@
             pltpu.VMEM((6, 26, 8, 128), F32),
             pltpu.SemaphoreType.DMA((2,)),
             pltpu.SemaphoreType.DMA((2,)),
-            pltpu.SemaphoreType.DMA((4,)),
-            pltpu.SemaphoreType.DMA((4,)),
+            pltpu.SemaphoreType.DMA((2,)),
+            pltpu.SemaphoreType.DMA((2,)),
+            pltpu.SemaphoreType.DMA((5,)),
+            pltpu.SemaphoreType.DMA((5,)),
+            pltpu.SemaphoreType.DMA((10,)),
         ],
         compiler_params=pltpu.CompilerParams(collective_id=0, has_side_effects=True),
         name="relax_letkf",
-    )(
-        ssh_prior, ssh_forcing, level_state, depth, damping, land_mask,
-        obs_column[0, 0], obs_value[0, 0], obs_weight[0, 0], obs_count[0, 0],
-    )
+    )(*operands)
+    return pl.pallas_call(
+        arrange,
+        grid=(2, 2),
+        out_shape=(
+            jax.ShapeDtypeStruct(ssh_prior.shape, F32),
+            jax.ShapeDtypeStruct(level_state.shape, F32),
+        ),
+        in_specs=[pl.BlockSpec((8, 1, 9, 8, 128), lambda o, h: (o, h, 0, 0, 0))],
+        out_specs=(
+            pl.BlockSpec((2, 8, 512), lambda o, h: (0, o, h)),
+            pl.BlockSpec((2, 8, 8, 512), lambda o, h: (0, 0, o, h)),
+        ),
+        name="arrange",
+    )(landed)
 
 
 def solution(mesh):

time: 132 us -> 128 us (0.970)
  the two profiles are of different devices: /device:TPU:24 before, /device:TPU:31 now
where the time goes in v2:
time: 128 us
  Pallas kernels  127 us (99%)
    pallas_call x1, Pallas kernels, local(): pl.pallas_call(functools.partial(kernel, mems, tiles), out_shape=jax.Shap...  124 us
    pallas_call x1, Pallas kernels, local(): pl.pallas_call(arrange, grid=(2, 2), out_shape=(jax.ShapeDtypeStruct(ssh_...  3.47 us

profile of v2, /device:TPU:31, one launch (start us, length us, event | category | flops | bytes accessed | tf_op | source)
XLA Modules:
  0.0 127.6 jit_solution(11339696197493575911)
XLA Ops:
  0.6 123.5 %relax_letkf.1.rb = f32[16,2,9,8,128]{4,3,2,1,0:T(8,128)} custom-call(f32[2,16,1024]{2,1,0:T(8,128)} %prior_hbm.1, f32[2,16,1024]{2,1,0:T(8,128)} %forcing_hbm.1, f32[2,8,16,1024]{3,2,1,0:T(8,128)} %levels_hbm.1, f32[16,1024]{1,0:T(8,128)} %depth_hbm.1, f32[16,1024]{1,0:T(8,128)} %damping_hbm.1, s32[16,1024]{1,0:T(8,128)} %mask_hbm.1, s32[4,128]{1,0:T(4,128)} %bitcast.4, ...), custom_call_target="tpu_custom_call" | custom-call | tf_op jit(solution)/shard_map/relax_letkf/pallas_call | solution.py:395
  124.2 3.5 %arrange.1 = (f32[2,16,1024]{2,1,0:T(8,128)}, f32[2,8,16,1024]{3,2,1,0:T(8,128)}) custom-call(f32[16,2,9,8,128]{4,3,2,1,0:T(8,128)} %relax_letkf.1.rb), custom_call_target="tpu_custom_call" | custom-call | tf_op jit(solution)/shard_map/arrange/pallas_call | solution.py:426

commit v3 on v2

--- a/solution.py
+++ b/solution.py
@@ -17,6 +17,8 @@
 PB, FR, FB, WR, WB, DR, DB, HALO = 0, 16, 32, 48, 56, 64, 72, 80
 QUARTER = HALO // 4
 FAR = 8
+SPAN = 8
+EARLY = 2
 FIRST = 4
 
 
@@ -36,7 +38,7 @@
     mems, tiles, prior_hbm, forcing_hbm, levels_hbm, depth_hbm, damping_hbm, mask_hbm, ocol_hbm, oval_hbm, owgt_hbm, ocnt_hbm, rb,
     prior, forcing, levels, depth, damping, mask, ocol, oval, owgt, ocnt,
     halo, relay, ls, lr, ss, sr, back, vr, vb, swr, swb, coef,
-    halo_send, halo_recv, relay_send, relay_recv, send, recv, fetch,
+    halo_send, halo_recv, relay_send, relay_recv, send, recv, fetch, phase, ready,
 ):
     me = lax.axis_index("mem")
     band = lax.axis_index("tile")
@@ -49,25 +51,50 @@
 
     barrier = pltpu.get_barrier_semaphore()
 
-    def greet(i, carry):
-        pl.semaphore_signal(barrier, inc=1, device_id={"mem": lax.rem(me + i, mems)}, device_id_type=MESH)
-        return carry
-
     def hail(role, *targets):
         @pl.when(role)
         def _():
             for target in targets:
                 pl.semaphore_signal(barrier, inc=1, device_id={"tile": target}, device_id_type=MESH)
 
-    lax.fori_loop(1, mems, greet, 0)
+    z = lax.rem(me, SPAN)
+    lower, upper = z > 0, z < SPAN - 1
+    lines = mems // SPAN
+
+    def peers(dz, first, visit):
+        def one(dy, carry):
+            visit(lax.rem(me + dz + SPAN * dy, mems))
+            return carry
+
+        lax.fori_loop(first, lines, one, 0)
+
+    def signal_mem(sem):
+        return lambda peer: pl.semaphore_signal(sem, inc=1, device_id={"mem": peer}, device_id_type=MESH)
+
+    def beside(k, visit):
+        @pl.when(z >= k)
+        def _():
+            peers(mems - k, 0, visit)
+
+        @pl.when(z + k < SPAN)
+        def _():
+            peers(k, 0, visit)
+
+    peers(0, 1, signal_mem(barrier))
+    beside(1, signal_mem(barrier))
     hail(near_north, band - 1)
     hail(near_south, band + 1)
     hail(above, 0, 2, 4, FAR + 7)
-    hail(below, 0, FAR + 2, FAR + 4, FAR + 7)
+    hail(below, FAR + 2, FAR + 4, FAR + 7)
     hail(low, FAR - 1, band + FAR)
-    hail(high, FAR, band - FAR)
-    greetings = mems - 1 + near_north.astype(jnp.int32) + near_south.astype(jnp.int32)
-    greetings += 4 * (above | below).astype(jnp.int32) + 2 * (low | high).astype(jnp.int32)
+    hail(high, FAR)
+
+    def count(*terms):
+        return sum(n * flag.astype(jnp.int32) for n, flag in terms)
+
+    greetings = lines - 1 + count(
+        (lines, lower), (lines, upper), (1, near_north), (1, near_south), (1, low), (3, above), (4, below), (2, high)
+    )
 
     fetches = [
         pltpu.make_async_copy(src, dst, fetch.at[n])
@@ -78,8 +105,6 @@
     ]
     for copy in fetches:
         copy.start()
-    for copy in fetches[:5]:
-        copy.wait()
 
     lane = lax.broadcasted_iota(jnp.int32, (8, 128), 1)
     sub = lax.broadcasted_iota(jnp.int32, (8, 128), 0)
@@ -87,6 +112,45 @@
     first_lane = (lane == 0)[None]
     last_lane = (lane == 127)[None]
     low_half = (sub < 4)[None]
+
+    fetches[5].wait()
+    for octet in range(2):
+        for b in range(8):
+            for a in range(2):
+                cut = levels[a, :, 8 * octet : 8 * octet + 8, 128 * b : 128 * b + 128]
+                ls[8 * octet : 8 * octet + 8, b // 4, 2 * (b % 4) + a] = jnp.swapaxes(cut, 0, 1)
+
+    pl.semaphore_wait(barrier, greetings)
+
+    def spread(k):
+        @pl.when(lower)
+        def _():
+            signal_mem(phase.at[k])(me - 1)
+
+        @pl.when(upper)
+        def _():
+            signal_mem(phase.at[k])(me + 1)
+
+    spread(2)
+
+    @pl.when((band == FAR) | high)
+    def _():
+        pl.semaphore_signal(ready, inc=1, device_id={"tile": lax.rem(band + FAR, tiles)}, device_id_type=MESH)
+
+    def ship(part, which):
+        def one(peer):
+            pltpu.make_async_remote_copy(
+                src_ref=ls.at[peer // 2, peer % 2, part], dst_ref=lr.at[me, part], send_sem=send.at[which],
+                recv_sem=recv.at[which], device_id={"mem": peer}, device_id_type=MESH,
+            ).start()
+
+        return one
+
+    early = ship(pl.ds(0, EARLY), 5)
+    peers(0, 1, early)
+    beside(1, early)
+    for copy in fetches[:5]:
+        copy.wait()
 
     def rows_first(x):
         parts = []
@@ -120,15 +184,6 @@
     def _():
         halo[2] = jnp.zeros((HALO, 8, 128), F32)
 
-    fetches[5].wait()
-    for octet in range(2):
-        for b in range(8):
-            for a in range(2):
-                cut = levels[a, :, 8 * octet : 8 * octet + 8, 128 * b : 128 * b + 128]
-                ls[8 * octet : 8 * octet + 8, b // 4, 2 * (b % 4) + a] = jnp.swapaxes(cut, 0, 1)
-
-    pl.semaphore_wait(barrier, greetings)
-
     to_south = pltpu.make_async_remote_copy(
         src_ref=halo.at[1], dst_ref=halo.at[0], send_sem=halo_send.at[0], recv_sem=halo_recv.at[0],
         device_id={"tile": lax.rem(band + 1, tiles)}, device_id_type=MESH,
@@ -153,7 +208,7 @@
 
     @pl.when(above)
     def _():
-        for q, target in enumerate((0, 2, 4, FAR + 7)):
+        for q, target in enumerate((0, 2, 4)):
             hand(halo.at[1, pl.ds(q * QUARTER, QUARTER)], relay.at[0], halo_send.at[0], relay_recv.at[0], target).start()
 
     @pl.when(below)
@@ -168,10 +223,31 @@
             pltpu.make_async_copy(relay.at[way], relay.at[way], relay_recv.at[way]).wait()
             copy.start()
 
+    pass_on(band == FAR + 7, 1, halo.at[2, quarter], halo_recv.at[1], FAR - 1)
+    pass_on((band == FAR + 2) | (band == FAR + 4), 1, relay.at[1], relay_recv.at[1], lax.rem(band + FAR, tiles))
+
+    def wave(k, carry):
+        pl.semaphore_wait(phase.at[k], count((1, lower), (1, upper)))
+
+        @pl.when(k < SPAN - 1)
+        def _():
+            spread(k + 1)
+
+        beside(k, early)
+        return carry
+
+    lax.fori_loop(2, SPAN, wave, 0)
+
+    @pl.when(above | low)
+    def _():
+        pl.semaphore_wait(ready, 1)
+
+    @pl.when(above)
+    def _():
+        hand(halo.at[1, pl.ds(3 * QUARTER, QUARTER)], relay.at[0], halo_send.at[0], relay_recv.at[0], FAR + 7).start()
+
     pass_on(band == 0, 0, halo.at[0, quarter], halo_recv.at[0], FAR)
     pass_on((band == 2) | (band == 4), 0, relay.at[0], relay_recv.at[0], lax.rem(band + FAR, tiles))
-    pass_on(band == FAR + 7, 1, halo.at[2, quarter], halo_recv.at[1], FAR - 1)
-    pass_on((band == FAR + 2) | (band == FAR + 4), 1, relay.at[1], relay_recv.at[1], lax.rem(band + FAR, tiles))
 
     def scatter(src_of, dst, which):
         def one(i, carry):
@@ -187,7 +263,7 @@
     def finish(ref, sem):
         pltpu.make_async_copy(ref, ref, sem).wait()
 
-    scatter(lambda p: ls.at[p // 2, p % 2, pl.ds(0, FIRST)], lr.at[me, pl.ds(0, FIRST)], 0)
+    scatter(lambda p: ls.at[p // 2, p % 2, pl.ds(EARLY, FIRST - EARLY)], lr.at[me, pl.ds(EARLY, FIRST - EARLY)], 0)
     lr[me] = ls[me // 2, me % 2]
 
     pass_on(high, 0, halo.at[0, quarter], halo_recv.at[0], FAR)
@@ -340,7 +416,8 @@
 
     for j in range(4):
         if j == 0:
-            finish(lr.at[pl.ds(0, mems - 1), pl.ds(0, FIRST)], recv.at[0])
+            finish(lr.at[pl.ds(0, mems - 1), pl.ds(0, EARLY)], recv.at[5])
+            finish(lr.at[pl.ds(0, mems - 1), pl.ds(EARLY, FIRST - EARLY)], recv.at[0])
         if 2 * j == FIRST:
             give(0, FIRST, 3)
             finish(lr.at[pl.ds(0, mems - 1), pl.ds(FIRST, 8 - FIRST)], recv.at[2])
@@ -362,25 +439,36 @@
     back[:, 8] = jnp.swapaxes(flat, 0, 1)
     give(FIRST, 9 - FIRST, 4)
 
-    finish(ls.at[pl.ds(0, 15), :, pl.ds(0, FIRST)], send.at[0])
-    finish(ls.at[0, 0, pl.ds(0, FIRST)], send.at[0])
     finish(ss.at[pl.ds(0, mems - 1)], send.at[1])
-    finish(ls.at[pl.ds(0, 15), :, pl.ds(FIRST, 8 - FIRST)], send.at[2])
-    finish(ls.at[0, 0, pl.ds(FIRST, 8 - FIRST)], send.at[2])
+    for which, part in ((5, pl.ds(0, EARLY)), (0, pl.ds(EARLY, FIRST - EARLY)), (2, pl.ds(FIRST, 8 - FIRST))):
+        finish(ls.at[pl.ds(0, 15), :, part], send.at[which])
+        finish(ls.at[0, 0, part], send.at[which])
     for which, part in ((3, pl.ds(0, FIRST)), (4, pl.ds(FIRST, 9 - FIRST))):
         pltpu.make_async_copy(back.at[me, part], rb.at[me // 2, me % 2, part], fetch.at[which]).wait()
         finish(back.at[pl.ds(0, mems - 1), part], send.at[which])
         finish(back.at[pl.ds(0, mems - 1), part], recv.at[which])
 
 
-def arrange(rb, outs, outl):
-    for j in range(4):
-        for a in range(2):
-            outl[a, :, :, 128 * j : 128 * j + 128] = jnp.swapaxes(rb[:, 0, 2 * j + a], 0, 1)
-    x = jnp.swapaxes(rb[:, 0, 8], 0, 1)
-    for j in range(4):
-        for a in range(2):
-            outs[a, :, 128 * j : 128 * j + 128] = x[4 * a + j]
+def arrange(rb, outs, outl, levels, surface, sems):
+    copies = []
+    for octet in range(2):
+        rows = slice(8 * octet, 8 * octet + 8)
+        for h in range(2):
+            left = slice(512 * h, 512 * h + 512)
+            for j in range(4):
+                for a in range(2):
+                    turned = jnp.swapaxes(rb[rows, h, 2 * j + a], 0, 1)
+                    levels[a, :, rows, 512 * h + 128 * j : 512 * h + 128 * j + 128] = turned
+            x = jnp.swapaxes(rb[rows, h, 8], 0, 1)
+            for j in range(4):
+                for a in range(2):
+                    surface[a, rows, 512 * h + 128 * j : 512 * h + 128 * j + 128] = x[4 * a + j]
+        copies.append(pltpu.make_async_copy(levels.at[:, :, rows], outl.at[:, :, rows], sems.at[octet]))
+        copies.append(pltpu.make_async_copy(surface.at[:, rows], outs.at[:, rows], sems.at[2 + octet]))
+        for copy in copies[2 * octet :]:
+            copy.start()
+    for copy in copies:
+        copy.wait()
 
 
 def local(
@@ -394,9 +482,9 @@
     anywhere = pl.BlockSpec(memory_space=pl.ANY)
     landed = pl.pallas_call(
         functools.partial(kernel, mems, tiles),
-        out_shape=jax.ShapeDtypeStruct((16, 2, 9, 8, 128), F32),
+        out_shape=pltpu.VMEM((16, 2, 9, 8, 128), F32),
         in_specs=[anywhere] * 10,
-        out_specs=anywhere,
+        out_specs=pl.BlockSpec(memory_space=pltpu.VMEM),
         scratch_shapes=[
             *(pltpu.VMEM(x.shape, x.dtype) for x in operands[:9]),
             pltpu.SMEM(operands[9].shape, operands[9].dtype),
@@ -416,27 +504,30 @@
             pltpu.SemaphoreType.DMA((2,)),
             pltpu.SemaphoreType.DMA((2,)),
             pltpu.SemaphoreType.DMA((2,)),
-            pltpu.SemaphoreType.DMA((5,)),
-            pltpu.SemaphoreType.DMA((5,)),
+            pltpu.SemaphoreType.DMA((6,)),
+            pltpu.SemaphoreType.DMA((6,)),
             pltpu.SemaphoreType.DMA((10,)),
+            pltpu.SemaphoreType.REGULAR((SPAN,)),
+            pltpu.SemaphoreType.REGULAR,
         ],
         compiler_params=pltpu.CompilerParams(collective_id=0, has_side_effects=True),
         name="relax_letkf",
     )(*operands)
     return pl.pallas_call(
         arrange,
-        grid=(2, 2),
         out_shape=(
             jax.ShapeDtypeStruct(ssh_prior.shape, F32),
             jax.ShapeDtypeStruct(level_state.shape, F32),
         ),
-        in_specs=[pl.BlockSpec((8, 1, 9, 8, 128), lambda o, h: (o, h, 0, 0, 0))],
-        out_specs=(
-            pl.BlockSpec((2, 8, 512), lambda o, h: (0, o, h)),
-            pl.BlockSpec((2, 8, 8, 512), lambda o, h: (0, 0, o, h)),
-        ),
+        in_specs=[pl.BlockSpec(memory_space=pltpu.VMEM)],
+        out_specs=(anywhere, anywhere),
+        scratch_shapes=[
+            pltpu.VMEM(level_state.shape, F32),
+            pltpu.VMEM(ssh_prior.shape, F32),
+            pltpu.SemaphoreType.DMA((4,)),
+        ],
         name="arrange",
-    )(landed)
+    )(pltpu.with_memory_space_constraint(landed, pltpu.VMEM))
 
 
 def solution(mesh):

time: 128 us -> 121 us (0.945)
  the two profiles are of different devices: /device:TPU:31 before, /device:TPU:1 now
where the time goes in v3:
time: 121 us
  Pallas kernels  121 us (100%)
    pallas_call x1, Pallas kernels, local(): pl.pallas_call(functools.partial(kernel, mems, tiles), out_shape=pltpu.VM...  120 us

profile of v3, /device:TPU:1, one launch (start us, length us, event | category | flops | bytes accessed | tf_op | source)
XLA Modules:
  0.0 121.3 jit_solution(14238585492045620798)
XLA Ops:
  0.6 119.6 %relax_letkf.1.rb = f32[16,2,9,8,128]{4,3,2,1,0:T(8,128)S(1)} custom-call(f32[2,16,1024]{2,1,0:T(8,128)} %prior_hbm.1, f32[2,16,1024]{2,1,0:T(8,128)} %forcing_hbm.1, f32[2,8,16,1024]{3,2,1,0:T(8,128)} %levels_hbm.1, f32[16,1024]{1,0:T(8,128)} %depth_hbm.1, f32[16,1024]{1,0:T(8,128)} %damping_hbm.1, s32[16,1024]{1,0:T(8,128)} %mask_hbm.1, s32[4,128]{1,0:T(4,128)} %bitcast.4, ...), custom_call_target="tpu_custom_call" | custom-call | tf_op jit(solution)/shard_map/relax_letkf/pallas_call | solution.py:483
  120.2 1.1 arrange.1

commit v4 on v3

--- a/solution.py
+++ b/solution.py
@@ -20,6 +20,7 @@
 SPAN = 8
 EARLY = 2
 FIRST = 4
+GIVES = (0, 4, 9)
 
 
 def split(x):
@@ -137,16 +138,19 @@
     def _():
         pl.semaphore_signal(ready, inc=1, device_id={"tile": lax.rem(band + FAR, tiles)}, device_id_type=MESH)
 
-    def ship(part, which):
+    def post(src_of, dst, which):
         def one(peer):
             pltpu.make_async_remote_copy(
-                src_ref=ls.at[peer // 2, peer % 2, part], dst_ref=lr.at[me, part], send_sem=send.at[which],
-                recv_sem=recv.at[which], device_id={"mem": peer}, device_id_type=MESH,
+                src_ref=src_of(peer), dst_ref=dst, send_sem=send.at[which], recv_sem=recv.at[which],
+                device_id={"mem": peer}, device_id_type=MESH,
             ).start()
 
         return one
 
-    early = ship(pl.ds(0, EARLY), 5)
+    def ship(part, which):
+        return post(lambda p: ls.at[p // 2, p % 2, part], lr.at[me, part], which)
+
+    early = ship(pl.ds(0, EARLY), 0)
     peers(0, 1, early)
     beside(1, early)
     for copy in fetches[:5]:
@@ -249,21 +253,21 @@
     pass_on(band == 0, 0, halo.at[0, quarter], halo_recv.at[0], FAR)
     pass_on((band == 2) | (band == 4), 0, relay.at[0], relay_recv.at[0], lax.rem(band + FAR, tiles))
 
-    def scatter(src_of, dst, which):
-        def one(i, carry):
-            peer = lax.rem(me + i, mems)
-            pltpu.make_async_remote_copy(
-                src_ref=src_of(peer), dst_ref=dst, send_sem=send.at[which], recv_sem=recv.at[which],
-                device_id={"mem": peer}, device_id_type=MESH,
-            ).start()
+    def everyone(visit):
+        def ring(i, carry):
+            beside(SPAN - i, visit)
             return carry
 
-        lax.fori_loop(1, mems, one, 0)
+        lax.fori_loop(1, SPAN, ring, 0)
+        peers(0, 1, visit)
 
     def finish(ref, sem):
         pltpu.make_async_copy(ref, ref, sem).wait()
 
-    scatter(lambda p: ls.at[p // 2, p % 2, pl.ds(EARLY, FIRST - EARLY)], lr.at[me, pl.ds(EARLY, FIRST - EARLY)], 0)
+    @pl.when(jnp.logical_not(above | below))
+    def _():
+        everyone(ship(pl.ds(EARLY, FIRST - EARLY), 1))
+
     lr[me] = ls[me // 2, me % 2]
 
     pass_on(high, 0, halo.at[0, quarter], halo_recv.at[0], FAR)
@@ -350,8 +354,13 @@
         halves.append(jnp.where(low_half, x0, pltpu.roll(x1, 4, 1)))
         halves.append(jnp.where(low_half, pltpu.roll(x0, 4, 1), x1))
     ss[...] = jnp.stack(halves, axis=1).reshape(mems, 8, 128)
-    scatter(lambda p: ss.at[p], sr.at[me], 1)
-    scatter(lambda p: ls.at[p // 2, p % 2, pl.ds(FIRST, 8 - FIRST)], lr.at[me, pl.ds(FIRST, 8 - FIRST)], 2)
+    everyone(post(lambda p: ss.at[p], sr.at[me], 3))
+
+    @pl.when(above | below)
+    def _():
+        everyone(ship(pl.ds(EARLY, FIRST - EARLY), 1))
+
+    everyone(ship(pl.ds(FIRST, 8 - FIRST), 2))
     sr[me] = ss[me]
 
     @pl.when(has_south)
@@ -371,7 +380,7 @@
         copy.wait()
 
     members = 2 * mems
-    finish(sr.at[pl.ds(0, mems - 1)], recv.at[1])
+    finish(sr.at[pl.ds(0, mems - 1)], recv.at[3])
     seen_all = jnp.swapaxes(sr[...], 0, 1)
     eye = (
         lax.broadcasted_iota(jnp.int32, (members, members), 0) == lax.broadcasted_iota(jnp.int32, (members, members), 1)
@@ -409,18 +418,17 @@
     for _ in range(NS_STEPS): state = iterate(0, state)
 
     tail = []
-    def give(first, count, which):
-        part = pl.ds(first, count)
-        scatter(lambda p: back.at[p, part], rb.at[me // 2, me % 2, part], which)
-        pltpu.make_async_copy(back.at[me, part], rb.at[me // 2, me % 2, part], fetch.at[which]).start()
-
+    def give(index):
+        first, last = GIVES[index : index + 2]
+        part = pl.ds(first, last - first)
+        everyone(post(lambda p: back.at[p, part], rb.at[me // 2, me % 2, part], 4 + index))
+        pltpu.make_async_copy(back.at[me, part], rb.at[me // 2, me % 2, part], fetch.at[index]).start()
+
+    groups = ((0, EARLY), (EARLY, FIRST), (FIRST, 8))
     for j in range(4):
-        if j == 0:
-            finish(lr.at[pl.ds(0, mems - 1), pl.ds(0, EARLY)], recv.at[5])
-            finish(lr.at[pl.ds(0, mems - 1), pl.ds(EARLY, FIRST - EARLY)], recv.at[0])
-        if 2 * j == FIRST:
-            give(0, FIRST, 3)
-            finish(lr.at[pl.ds(0, mems - 1), pl.ds(FIRST, 8 - FIRST)], recv.at[2])
+        for which, (first, last) in enumerate(groups):
+            if first // 2 == j and last > first:
+                finish(lr.at[pl.ds(0, mems - 1), pl.ds(first, last - first)], recv.at[which])
         root = state[2 * j + 1]
         inner = jnp.sum(root * drive[j], axis=1, keepdims=True)
         mean_w = jnp.sum(root * inner, axis=0, keepdims=True) / traces[j]
@@ -435,18 +443,23 @@
             piece = jnp.stack([y[mems * a : mems * a + mems, 128 * l : 128 * l + 128] for l in range(8)], axis=0)
             back[:, 2 * j + a] = jnp.swapaxes(piece, 0, 1)
         tail.append([y[0:mems, 1024:1152], y[mems:members, 1024:1152]])
+        if 2 * j + 2 in GIVES[:-1]:
+            give(GIVES.index(2 * j + 2) - 1)
     flat = jnp.stack([tail[j][a] for a in range(2) for j in range(4)], axis=0)
     back[:, 8] = jnp.swapaxes(flat, 0, 1)
-    give(FIRST, 9 - FIRST, 4)
-
-    finish(ss.at[pl.ds(0, mems - 1)], send.at[1])
-    for which, part in ((5, pl.ds(0, EARLY)), (0, pl.ds(EARLY, FIRST - EARLY)), (2, pl.ds(FIRST, 8 - FIRST))):
+    give(len(GIVES) - 2)
+
+    finish(ss.at[pl.ds(0, mems - 1)], send.at[3])
+    for which, (first, last) in enumerate(groups):
+        part = pl.ds(first, last - first)
         finish(ls.at[pl.ds(0, 15), :, part], send.at[which])
         finish(ls.at[0, 0, part], send.at[which])
-    for which, part in ((3, pl.ds(0, FIRST)), (4, pl.ds(FIRST, 9 - FIRST))):
-        pltpu.make_async_copy(back.at[me, part], rb.at[me // 2, me % 2, part], fetch.at[which]).wait()
-        finish(back.at[pl.ds(0, mems - 1), part], send.at[which])
-        finish(back.at[pl.ds(0, mems - 1), part], recv.at[which])
+    for index in range(len(GIVES) - 1):
+        first, last = GIVES[index : index + 2]
+        part = pl.ds(first, last - first)
+        pltpu.make_async_copy(back.at[me, part], rb.at[me // 2, me % 2, part], fetch.at[index]).wait()
+        finish(back.at[pl.ds(0, mems - 1), part], send.at[4 + index])
+        finish(back.at[pl.ds(0, mems - 1), part], recv.at[4 + index])
 
 
 def arrange(rb, outs, outl, levels, surface, sems):
@@ -504,8 +517,8 @@
             pltpu.SemaphoreType.DMA((2,)),
             pltpu.SemaphoreType.DMA((2,)),
             pltpu.SemaphoreType.DMA((2,)),
-            pltpu.SemaphoreType.DMA((6,)),
-            pltpu.SemaphoreType.DMA((6,)),
+            pltpu.SemaphoreType.DMA((3 + len(GIVES),)),
+            pltpu.SemaphoreType.DMA((3 + len(GIVES),)),
             pltpu.SemaphoreType.DMA((10,)),
             pltpu.SemaphoreType.REGULAR((SPAN,)),
             pltpu.SemaphoreType.REGULAR,

time: 121 us -> 120 us (level); the launches traced: 121 us -> 117 us
  Pallas kernels: 121 us -> 117 us
    pallas_call x1, Pallas kernels: 120 us -> 116 us  [local(): pl.pallas_call(functools.partial(kernel, mems, tiles), out_shape=pltpu.VM...]
where the time goes in v4:
time: 120 us; the launch traced here: 117 us
  Pallas kernels  117 us (98%)
    pallas_call x1, Pallas kernels, local(): pl.pallas_call(functools.partial(kernel, mems, tiles), out_shape=pltpu.VM...  116 us

profile of v4, /device:TPU:1, one launch (start us, length us, event | category | flops | bytes accessed | tf_op | source)
XLA Modules:
  0.0 117.4 jit_solution(5619050962155505847)
XLA Ops:
  0.6 115.6 %relax_letkf.1.rb = f32[16,2,9,8,128]{4,3,2,1,0:T(8,128)S(1)} custom-call(f32[2,16,1024]{2,1,0:T(8,128)} %prior_hbm.1, f32[2,16,1024]{2,1,0:T(8,128)} %forcing_hbm.1, f32[2,8,16,1024]{3,2,1,0:T(8,128)} %levels_hbm.1, f32[16,1024]{1,0:T(8,128)} %depth_hbm.1, f32[16,1024]{1,0:T(8,128)} %damping_hbm.1, s32[16,1024]{1,0:T(8,128)} %mask_hbm.1, s32[4,128]{1,0:T(4,128)} %bitcast.4, ...), custom_call_target="tpu_custom_call" | custom-call | tf_op jit(solution)/shard_map/relax_letkf/pallas_call | solution.py:496
  116.2 1.1 arrange.1

commit v5 on v4

--- a/solution.py
+++ b/solution.py
@@ -104,7 +104,7 @@
             (levels_hbm, levels), (ocol_hbm, ocol), (oval_hbm, oval), (owgt_hbm, owgt), (ocnt_hbm, ocnt),
         ))
     ]
-    for copy in fetches:
+    for copy in (fetches[5], *fetches[:5], *fetches[6:]):
         copy.start()
 
     lane = lax.broadcasted_iota(jnp.int32, (8, 128), 1)

time: 120 us -> 120 us (level)
  no operation moved by 1% of the time
where the time goes in v5:
time: 120 us; the launch traced here: 117 us
  Pallas kernels  117 us (98%)
    pallas_call x1, Pallas kernels, local(): pl.pallas_call(functools.partial(kernel, mems, tiles), out_shape=pltpu.VM...  116 us

profile of v5, /device:TPU:1, one launch (start us, length us, event | category | flops | bytes accessed | tf_op | source)
XLA Modules:
  0.0 117.4 jit_solution(10044995020112686174)
XLA Ops:
  0.6 115.6 %relax_letkf.1.rb = f32[16,2,9,8,128]{4,3,2,1,0:T(8,128)S(1)} custom-call(f32[2,16,1024]{2,1,0:T(8,128)} %prior_hbm.1, f32[2,16,1024]{2,1,0:T(8,128)} %forcing_hbm.1, f32[2,8,16,1024]{3,2,1,0:T(8,128)} %levels_hbm.1, f32[16,1024]{1,0:T(8,128)} %depth_hbm.1, f32[16,1024]{1,0:T(8,128)} %damping_hbm.1, s32[16,1024]{1,0:T(8,128)} %mask_hbm.1, s32[4,128]{1,0:T(4,128)} %bitcast.4, ...), custom_call_target="tpu_custom_call" | custom-call | tf_op jit(solution)/shard_map/relax_letkf/pallas_call | solution.py:496
  116.2 1.1 arrange.1
